TPU v7x, 32 devices: a whole 2x2x4 slice. The times are simulated.
32 devices in a mesh: slab: 2 (over y), row: 8 (over z, x), col: 2 (over core).
Axes of the slice: x: 2, y: 2, z: 4, core: 2. Of those that a mesh axis runs over, the one named last changes fastest.
Arguments:
- radiance: bfloat16 [16, 256, 256], P('slab', 'row', 'col'), parts along dimension 0, may hold values from -6 to 6
- sky_view: bfloat16 [32, 256, 256], P('slab', 'row', 'col'), parts along dimension 0, may hold values from 0.19921875 to 1
- tap_weight: float32 [33, 33], replicated, may hold values from 0.01 to 0.1
- tap_sector: int32 [33, 33], replicated, may hold values from 0 to 15
- far_weight: float32 [33, 33], replicated, may hold values from 0.08 to 0.8
- land_mask: int32 [16, 2], P(('slab', 'row'), 'col'), parts along dimension 0, may hold values 0 or 1
Outputs:
- reflected: bfloat16 [16, 256, 256], P('slab', 'row', 'col'), parts along dimension 0
There are 2 independent parts, one for each index of `slab`. A program takes and returns all parts, laid end to end along the dimension named above; an argument that names none is the same for every part. Nothing has to cross between parts.
All inputs are finite; a program needn't handle non-finite values. No bound on the sum of `land_mask` on one device may be relied on, other than what follows from the above.
Results may differ from a plain program's by a relative error of at most 0.012.
Values may be sent and summed in bfloat16 or wider, within the bound.
No kernel may reach another device: no remote copies, remote signals or barrier semaphores. Data moves between devices by JAX's collectives and lax.ppermute only.
A program may use at most 64 MiB of HBM per device.

v0:
```python
import jax
import jax.numpy as jnp
from jax import lax
from jax.sharding import PartitionSpec as P

DEC = 16


def extended_2(cells, sides, width):
    for axis, dim in sides:
        count = lax.axis_size(axis)
        ends = count - 1
        head = lax.slice_in_dim(cells, 0, width, axis=dim)
        tail = lax.slice_in_dim(cells, cells.shape[dim] - width, cells.shape[dim], axis=dim)
        cells = jnp.concatenate(
            [
                lax.ppermute(tail, axis, [(i, (i + 1) % count) for i in range(ends)]),
                cells,
                lax.ppermute(head, axis, [((i + 1) % count, i) for i in range(ends)]),
            ],
            axis=dim,
        )
    return cells


def shifted_2(value, axis, steps):
    count = lax.axis_size(axis)
    leading, last = (max(0, -steps), min(count, count - steps))
    return lax.ppermute(value, axis, [(source, source + steps) for source in range(leading, last)])


def shrink(portion):
    band_count, row_count, col_count = portion.shape
    blocks = portion.astype(jnp.float32).reshape(
        band_count, row_count // DEC, DEC, col_count // DEC, DEC
    )
    return jnp.mean(blocks, axis=(2, 4)).astype(jnp.bfloat16)


def near_field(extended, sky_view, kernels):
    sector_count, row_count, col_count = sky_view.shape
    band_count = extended.shape[0]
    span = kernels.shape[1]
    wide_cols = extended.shape[2]
    group = 1
    for candidate in range(1, 9):
        if span % candidate == 0:
            group = candidate
    source_col = jnp.arange(wide_cols, dtype=jnp.int32)[:, None, None]
    target_col = jnp.arange(col_count, dtype=jnp.int32)[None, :, None]
    offsets = jnp.arange(span, dtype=jnp.int32)[None, None, :]
    onehot = (source_col - target_col == offsets).astype(jnp.bfloat16)

    def add_rows(step, total):
        first = step * group
        kernel_rows = lax.dynamic_slice_in_dim(kernels, first, group, 1)
        banded = jnp.einsum(
            "cjd,sad->acsj", onehot, kernel_rows, preferred_element_type=jnp.float32
        ).astype(jnp.bfloat16)
        banded = banded.reshape(group * wide_cols, sector_count * col_count)
        shifted = jnp.stack(
            [lax.dynamic_slice_in_dim(extended, first + k, row_count, 1) for k in range(group)],
            axis=2,
        )
        shifted = shifted.reshape(band_count * row_count, group * wide_cols)
        return total + jnp.dot(shifted, banded, preferred_element_type=jnp.float32)

    empty = jnp.zeros((band_count * row_count, sector_count * col_count), jnp.float32)
    sector_sums = lax.fori_loop(0, span // group, add_rows, empty)
    sector_sums = sector_sums.reshape(band_count, row_count, sector_count, col_count)
    return jnp.einsum("bisj,sij->bij", sector_sums, sky_view.astype(jnp.float32))


def sea_field(extended, sky_view, kernels):
    sector_count, row_count, col_count = sky_view.shape
    return jnp.zeros((extended.shape[0], row_count, col_count), jnp.float32)


def body(radiance, sky_view, tap_weight, tap_sector, far_weight, land_mask):
    band_count, row_count, col_count = radiance.shape
    sector_count = sky_view.shape[0]
    near_reach = (tap_weight.shape[0] - 1) // 2
    far_reach = (far_weight.shape[0] - 1) // 2
    extended = extended_2(radiance, (("row", 1), ("col", 2)), near_reach)
    selector = tap_sector[None] == jnp.arange(sector_count, dtype=jnp.int32)[:, None, None]
    kernels = jnp.where(selector, tap_weight[None], 0.0).astype(jnp.bfloat16)
    near_total = lax.cond(land_mask[0, 0] > 0, near_field, sea_field, extended, sky_view, kernels)
    coarse_rows = row_count // DEC
    coarse_cols = col_count // DEC
    hop_count = far_reach // coarse_rows
    live_hops = min(hop_count, lax.axis_size("row") - 1)
    own_piece = shrink(radiance)
    coarse_band = jnp.zeros((2 * hop_count + 1,) + own_piece.shape, jnp.bfloat16)
    coarse_band = coarse_band.at[hop_count].set(own_piece)

    def advance(k, carry):
        lower_piece, upper_piece, gathered = carry
        lower_piece = shifted_2(lower_piece, "row", 1)
        upper_piece = shifted_2(upper_piece, "row", -1)
        gathered = lax.dynamic_update_index_in_dim(gathered, lower_piece, hop_count - k, 0)
        gathered = lax.dynamic_update_index_in_dim(gathered, upper_piece, hop_count + k, 0)
        return (lower_piece, upper_piece, gathered)

    carried = lax.fori_loop(1, live_hops + 1, advance, (own_piece, own_piece, coarse_band))
    coarse_band = carried[2]
    coarse_band = jnp.transpose(coarse_band, (1, 0, 2, 3)).reshape(
        band_count, -1, coarse_band.shape[3]
    )
    coarse_band = lax.all_gather(coarse_band, "col", axis=2, tiled=True)
    full_cols = coarse_band.shape[2]
    col_first = lax.axis_index("col") * coarse_cols
    column_weights = jnp.stack(
        [
            lax.dynamic_slice_in_dim(far_weight, far_reach - col_first - j, full_cols, 1)
            for j in range(coarse_cols)
        ]
    )
    window = 2 * far_reach + 1
    row_windows = jnp.stack([coarse_band[:, i : i + window, :] for i in range(coarse_rows)]).astype(
        jnp.float32
    )
    far_cells = jnp.einsum(
        "ibac,jac->bij", row_windows, column_weights, precision=lax.Precision.HIGHEST
    )
    far_fine = jnp.repeat(jnp.repeat(far_cells, DEC, axis=1), DEC, axis=2)
    total = jnp.where(land_mask[0, 0] > 0, near_total + far_fine, 0.0)
    return total.astype(jnp.bfloat16)


def solution(mesh):
    in_specs = (
        P("slab", "row", "col"),
        P("slab", "row", "col"),
        P(),
        P(),
        P(),
        P(("slab", "row"), "col"),
    )
    out_specs = P("slab", "row", "col")
    return jax.shard_map(body, mesh=mesh, in_specs=in_specs, out_specs=out_specs, check_vma=False)
```

profile of v0, /device:TPU:0, one launch (start us, length us, event | category | flops | bytes accessed | tf_op | source)
XLA Modules:
  0.0 144.4 jit_solution(7330245996405641891)
XLA Ops:
  0.0 0.8 fusion.19
  0.8 4.9 %collective-permute-start.2 = (bf16[8,16,128]{2,1,0:T(8,128)(2,1)S(1)}, bf16[8,16,128]{2,1,0:T(8,128)(2,1)S(1)}, u32[]{:S(2)}, u32[]{:S(2)}) collective-permute-start(bf16[8,16,128]{2,1,0:T(8,128)(2,1)S(1)} %get-tuple-element.298), channel_id=1, source_target_pairs={{0,2},{2,4},{4,6},{6,8},{8,10},{10,12},{12,14},{1,3},{3,5},{5,7},{... | collective-permute-start | bytes 98312 | tf_op jit(solution)/shard_map/ppermute | solution.py:17
  5.7 1.3 collective-permute-start.3
  7.0 1.1 reshape.109
  8.4 66.9 %while.34 = (s32[]{:T(128)}, bf16[8,2,8]{2,0,1:T(8,128)(2,1)S(1)}, bf16[8,2,8]{2,0,1:T(8,128)(2,1)S(1)}, bf16[17,8,2,8]{3,1,2,0:T(8,128)(2,1)S(1)}, s32[]{:T(128...) while((s32[]{:T(128)}, bf16[8,2,8]{2,0,1:T(8,128)(2,1)S(1)}, ...), condition=%wide.region_6.7_spmd, body=%wide.region_5.6_spmd.sunk | while | flops 10 | bytes 19745 | solution.py:104
  8.4 4.5 %collective-permute-start = (bf16[8,2,8]{2,0,1:T(8,128)(2,1)S(1)}, bf16[8,2,8]{2,0,1:T(8,128)(2,1)S(1)}, u32[]{:S(2)}, u32[]{:S(2)}) collective-permute-start(bf16[8,2,8]{2,0,1:T(8,128)(2,1)S(1)} %get-tuple-element.425), channel_id=1, source_target_pairs={{0,2},{2,4},{4,6},{6,8},{8,10},{10,12},{12,14},{1,3},{3,5},{5,7},{... | collective-permute-start | bytes 776 | tf_op jit(solution)/shard_map/while/body/eval_jaxpr/ppermute | solution.py:29
  12.9 1.3 collective-permute-start.1
  14.3 4.6 %collective-permute-done.1 = bf16[8,2,8]{2,0,1:T(8,128)(2,1)S(1)} collective-permute-done((bf16[8,2,8]{2,0,1:T(8,128)(2,1)S(1)}, bf16[8,2,8]{2,0,1:T(8,128)(2,1)S(1)}, u32[]{:S(2)}, u32[]{:S(2)}) %collective-permute-start.1) | collective-permute-done | bytes 288 | tf_op jit(solution)/shard_map/while/body/eval_jaxpr/ppermute | solution.py:29
  18.9 4.8 %collective-permute-start = (bf16[8,2,8]{2,0,1:T(8,128)(2,1)S(1)}, bf16[8,2,8]{2,0,1:T(8,128)(2,1)S(1)}, u32[]{:S(2)}, u32[]{:S(2)}) collective-permute-start(bf16[8,2,8]{2,0,1:T(8,128)(2,1)S(1)} %get-tuple-element.425), channel_id=1, source_target_pairs={{0,2},{2,4},{4,6},{6,8},{8,10},{10,12},{12,14},{1,3},{3,5},{5,7},{... | collective-permute-start | bytes 776 | tf_op jit(solution)/shard_map/while/body/eval_jaxpr/ppermute | solution.py:29
  23.7 1.3 collective-permute-start.1
  25.1 4.2 %collective-permute-done.1 = bf16[8,2,8]{2,0,1:T(8,128)(2,1)S(1)} collective-permute-done((bf16[8,2,8]{2,0,1:T(8,128)(2,1)S(1)}, bf16[8,2,8]{2,0,1:T(8,128)(2,1)S(1)}, u32[]{:S(2)}, u32[]{:S(2)}) %collective-permute-start.1) | collective-permute-done | bytes 288 | tf_op jit(solution)/shard_map/while/body/eval_jaxpr/ppermute | solution.py:29
  29.2 2.9 %collective-permute-start = (bf16[8,2,8]{2,0,1:T(8,128)(2,1)S(1)}, bf16[8,2,8]{2,0,1:T(8,128)(2,1)S(1)}, u32[]{:S(2)}, u32[]{:S(2)}) collective-permute-start(bf16[8,2,8]{2,0,1:T(8,128)(2,1)S(1)} %get-tuple-element.425), channel_id=1, source_target_pairs={{0,2},{2,4},{4,6},{6,8},{8,10},{10,12},{12,14},{1,3},{3,5},{5,7},{... | collective-permute-start | bytes 776 | tf_op jit(solution)/shard_map/while/body/eval_jaxpr/ppermute | solution.py:29
  32.2 1.3 collective-permute-start.1
  33.5 4.2 %collective-permute-done.1 = bf16[8,2,8]{2,0,1:T(8,128)(2,1)S(1)} collective-permute-done((bf16[8,2,8]{2,0,1:T(8,128)(2,1)S(1)}, bf16[8,2,8]{2,0,1:T(8,128)(2,1)S(1)}, u32[]{:S(2)}, u32[]{:S(2)}) %collective-permute-start.1) | collective-permute-done | bytes 288 | tf_op jit(solution)/shard_map/while/body/eval_jaxpr/ppermute | solution.py:29
  37.7 4.8 %collective-permute-start = (bf16[8,2,8]{2,0,1:T(8,128)(2,1)S(1)}, bf16[8,2,8]{2,0,1:T(8,128)(2,1)S(1)}, u32[]{:S(2)}, u32[]{:S(2)}) collective-permute-start(bf16[8,2,8]{2,0,1:T(8,128)(2,1)S(1)} %get-tuple-element.425), channel_id=1, source_target_pairs={{0,2},{2,4},{4,6},{6,8},{8,10},{10,12},{12,14},{1,3},{3,5},{5,7},{... | collective-permute-start | bytes 776 | tf_op jit(solution)/shard_map/while/body/eval_jaxpr/ppermute | solution.py:29
  42.5 1.3 collective-permute-start.1
  43.9 4.2 %collective-permute-done.1 = bf16[8,2,8]{2,0,1:T(8,128)(2,1)S(1)} collective-permute-done((bf16[8,2,8]{2,0,1:T(8,128)(2,1)S(1)}, bf16[8,2,8]{2,0,1:T(8,128)(2,1)S(1)}, u32[]{:S(2)}, u32[]{:S(2)}) %collective-permute-start.1) | collective-permute-done | bytes 288 | tf_op jit(solution)/shard_map/while/body/eval_jaxpr/ppermute | solution.py:29
  48.1 2.9 %collective-permute-start = (bf16[8,2,8]{2,0,1:T(8,128)(2,1)S(1)}, bf16[8,2,8]{2,0,1:T(8,128)(2,1)S(1)}, u32[]{:S(2)}, u32[]{:S(2)}) collective-permute-start(bf16[8,2,8]{2,0,1:T(8,128)(2,1)S(1)} %get-tuple-element.425), channel_id=1, source_target_pairs={{0,2},{2,4},{4,6},{6,8},{8,10},{10,12},{12,14},{1,3},{3,5},{5,7},{... | collective-permute-start | bytes 776 | tf_op jit(solution)/shard_map/while/body/eval_jaxpr/ppermute | solution.py:29
  51.0 1.3 collective-permute-start.1
  52.3 4.2 %collective-permute-done.1 = bf16[8,2,8]{2,0,1:T(8,128)(2,1)S(1)} collective-permute-done((bf16[8,2,8]{2,0,1:T(8,128)(2,1)S(1)}, bf16[8,2,8]{2,0,1:T(8,128)(2,1)S(1)}, u32[]{:S(2)}, u32[]{:S(2)}) %collective-permute-start.1) | collective-permute-done | bytes 288 | tf_op jit(solution)/shard_map/while/body/eval_jaxpr/ppermute | solution.py:29
  56.5 4.8 %collective-permute-start = (bf16[8,2,8]{2,0,1:T(8,128)(2,1)S(1)}, bf16[8,2,8]{2,0,1:T(8,128)(2,1)S(1)}, u32[]{:S(2)}, u32[]{:S(2)}) collective-permute-start(bf16[8,2,8]{2,0,1:T(8,128)(2,1)S(1)} %get-tuple-element.425), channel_id=1, source_target_pairs={{0,2},{2,4},{4,6},{6,8},{8,10},{10,12},{12,14},{1,3},{3,5},{5,7},{... | collective-permute-start | bytes 776 | tf_op jit(solution)/shard_map/while/body/eval_jaxpr/ppermute | solution.py:29
  61.4 1.3 collective-permute-start.1
  62.7 4.2 %collective-permute-done.1 = bf16[8,2,8]{2,0,1:T(8,128)(2,1)S(1)} collective-permute-done((bf16[8,2,8]{2,0,1:T(8,128)(2,1)S(1)}, bf16[8,2,8]{2,0,1:T(8,128)(2,1)S(1)}, u32[]{:S(2)}, u32[]{:S(2)}) %collective-permute-start.1) | collective-permute-done | bytes 288 | tf_op jit(solution)/shard_map/while/body/eval_jaxpr/ppermute | solution.py:29
  66.9 2.8 %collective-permute-start = (bf16[8,2,8]{2,0,1:T(8,128)(2,1)S(1)}, bf16[8,2,8]{2,0,1:T(8,128)(2,1)S(1)}, u32[]{:S(2)}, u32[]{:S(2)}) collective-permute-start(bf16[8,2,8]{2,0,1:T(8,128)(2,1)S(1)} %get-tuple-element.425), channel_id=1, source_target_pairs={{0,2},{2,4},{4,6},{6,8},{8,10},{10,12},{12,14},{1,3},{3,5},{5,7},{... | collective-permute-start | bytes 776 | tf_op jit(solution)/shard_map/while/body/eval_jaxpr/ppermute | solution.py:29
  69.7 1.3 collective-permute-start.1
  71.0 4.2 %collective-permute-done.1 = bf16[8,2,8]{2,0,1:T(8,128)(2,1)S(1)} collective-permute-done((bf16[8,2,8]{2,0,1:T(8,128)(2,1)S(1)}, bf16[8,2,8]{2,0,1:T(8,128)(2,1)S(1)}, u32[]{:S(2)}, u32[]{:S(2)}) %collective-permute-start.1) | collective-permute-done | bytes 288 | tf_op jit(solution)/shard_map/while/body/eval_jaxpr/ppermute | solution.py:29
  75.4 1.8 %all_gather.3 = bf16[8,34,16]{1,0,2:T(8,128)(2,1)S(1)} all-gather(bf16[8,34,8]{1,0,2:T(8,128)(2,1)S(1)} %copy.72), channel_id=1, replica_groups=mesh['slab'=2,'row'=8,'col'=2] {'col'}, dimensions={2}, use_global_device_ids=true | all-gather | bytes 13056 | tf_op jit(solution)/shard_map/all_gather | solution.py:109
  78.4 2.1 %collective-permute-start.4 = (bf16[8,64,16]{2,1,0:T(8,128)(2,1)S(1)}, bf16[8,64,16]{2,1,0:T(8,128)(2,1)S(1)}, u32[]{:S(2)}, u32[]{:S(2)}) collective-permute-start(bf16[8,64,16]{2,1,0:T(8,128)(2,1)S(1)} %get-tuple-element.295), channel_id=1, source_target_pairs={{0,1},{2,3},{4,5},{6,7},{8,9},{10,11},{12,13},{14,15},{16,17},{18,... | collective-permute-start | bytes 49160 | tf_op jit(solution)/shard_map/ppermute | solution.py:17
  80.5 1.3 collective-permute-start.5
  83.9 59.9 %conditional.1 = (f32[8,32,128]{2,1,0:T(8,128)S(1)}) conditional(s32[]{:T(128)} %convert_element_type.39, () %tuple.51, (bf16[8,64,160]{2,1,0:T(8,128)(2,1)S(1)}, bf16[16,33,33]{2,0,1:T(8,128)(2,1)S(1)}, bf16[16,32,128]{2,1,0:T(8,128)(2,1)S(1)}) %tuple.102), branch_computations={%region_0.1_spmd, %region_1.4_spmd} | conditional | flops 572928000 | bytes 18117042 | solution.py:87
  84.0 57.1 %while.33 = (s32[]{:T(128)}, f32[256,2048]{1,0:T(8,128)}, bf16[8,64,160]{2,1,0:T(8,128)(2,1)S(1)}, bf16[16,33,33]{2,0,1:T(8,128)(2,1)S(1)}, s32[160,128]{1,0:T(8...) while((s32[]{:T(128)}, f32[256,2048]{1,0:T(8,128)}, ...), condition=%wide.region_3.3_spmd.clone, body=%wide.region_2.2_spmd.clone.sunk | while | flops 571826176 | bytes 10432826 | solution.py:69
  84.9 0.7 convolution_convert_fusion.2
  85.6 2.1 %convolution_add_fusion.2 = f32[256,2048]{1,0:T(8,128)} fusion(bf16[256,480]{1,0:T(8,128)(2,1)S(1)} %reshape.119, f32[256,2048]{1,0:T(8,128)} %get-tuple-element.387, bf16[60,8,16,128]{3,2,1,0:T(8,128)(2,1)S(1)} %bitcast.90, pred[]{:T(512)S(6)} %compare.9), kind=kOutput, calls=%fused_computation.5.clone.1 | convolution fusion | flops 504365056 | bytes 6406145 | tf_op jit(solution)/shard_map/cond/branch_1_fun/while/body/eval_jaxpr/dot_general | solution.py:66
  89.4 3.7 %convolution_add_fusion.2 = f32[256,2048]{1,0:T(8,128)} fusion(bf16[256,480]{1,0:T(8,128)(2,1)S(1)} %reshape.119, f32[256,2048]{1,0:T(8,128)} %get-tuple-element.387, bf16[60,8,16,128]{3,2,1,0:T(8,128)(2,1)S(1)} %bitcast.90, pred[]{:T(512)S(6)} %compare.9), kind=kOutput, calls=%fused_computation.5.clone.1 | convolution fusion | flops 504365056 | bytes 6406145 | tf_op jit(solution)/shard_map/cond/branch_1_fun/while/body/eval_jaxpr/dot_general | solution.py:66
  94.0 0.7 convolution_convert_fusion.2
  94.7 3.7 %convolution_add_fusion.2 = f32[256,2048]{1,0:T(8,128)} fusion(bf16[256,480]{1,0:T(8,128)(2,1)S(1)} %reshape.119, f32[256,2048]{1,0:T(8,128)} %get-tuple-element.387, bf16[60,8,16,128]{3,2,1,0:T(8,128)(2,1)S(1)} %bitcast.90, pred[]{:T(512)S(6)} %compare.9), kind=kOutput, calls=%fused_computation.5.clone.1 | convolution fusion | flops 504365056 | bytes 6406145 | tf_op jit(solution)/shard_map/cond/branch_1_fun/while/body/eval_jaxpr/dot_general | solution.py:66
  99.3 0.7 convolution_convert_fusion.2
  100.0 3.7 %convolution_add_fusion.2 = f32[256,2048]{1,0:T(8,128)} fusion(bf16[256,480]{1,0:T(8,128)(2,1)S(1)} %reshape.119, f32[256,2048]{1,0:T(8,128)} %get-tuple-element.387, bf16[60,8,16,128]{3,2,1,0:T(8,128)(2,1)S(1)} %bitcast.90, pred[]{:T(512)S(6)} %compare.9), kind=kOutput, calls=%fused_computation.5.clone.1 | convolution fusion | flops 504365056 | bytes 6406145 | tf_op jit(solution)/shard_map/cond/branch_1_fun/while/body/eval_jaxpr/dot_general | solution.py:66
  105.4 3.7 %convolution_add_fusion.2 = f32[256,2048]{1,0:T(8,128)} fusion(bf16[256,480]{1,0:T(8,128)(2,1)S(1)} %reshape.119, f32[256,2048]{1,0:T(8,128)} %get-tuple-element.387, bf16[60,8,16,128]{3,2,1,0:T(8,128)(2,1)S(1)} %bitcast.90, pred[]{:T(512)S(6)} %compare.9), kind=kOutput, calls=%fused_computation.5.clone.1 | convolution fusion | flops 504365056 | bytes 6406145 | tf_op jit(solution)/shard_map/cond/branch_1_fun/while/body/eval_jaxpr/dot_general | solution.py:66
  110.7 3.7 %convolution_add_fusion.2 = f32[256,2048]{1,0:T(8,128)} fusion(bf16[256,480]{1,0:T(8,128)(2,1)S(1)} %reshape.119, f32[256,2048]{1,0:T(8,128)} %get-tuple-element.387, bf16[60,8,16,128]{3,2,1,0:T(8,128)(2,1)S(1)} %bitcast.90, pred[]{:T(512)S(6)} %compare.9), kind=kOutput, calls=%fused_computation.5.clone.1 | convolution fusion | flops 504365056 | bytes 6406145 | tf_op jit(solution)/shard_map/cond/branch_1_fun/while/body/eval_jaxpr/dot_general | solution.py:66
  115.3 0.7 convolution_convert_fusion.2
  116.0 3.7 %convolution_add_fusion.2 = f32[256,2048]{1,0:T(8,128)} fusion(bf16[256,480]{1,0:T(8,128)(2,1)S(1)} %reshape.119, f32[256,2048]{1,0:T(8,128)} %get-tuple-element.387, bf16[60,8,16,128]{3,2,1,0:T(8,128)(2,1)S(1)} %bitcast.90, pred[]{:T(512)S(6)} %compare.9), kind=kOutput, calls=%fused_computation.5.clone.1 | convolution fusion | flops 504365056 | bytes 6406145 | tf_op jit(solution)/shard_map/cond/branch_1_fun/while/body/eval_jaxpr/dot_general | solution.py:66
  121.4 3.7 %convolution_add_fusion.2 = f32[256,2048]{1,0:T(8,128)} fusion(bf16[256,480]{1,0:T(8,128)(2,1)S(1)} %reshape.119, f32[256,2048]{1,0:T(8,128)} %get-tuple-element.387, bf16[60,8,16,128]{3,2,1,0:T(8,128)(2,1)S(1)} %bitcast.90, pred[]{:T(512)S(6)} %compare.9), kind=kOutput, calls=%fused_computation.5.clone.1 | convolution fusion | flops 504365056 | bytes 6406145 | tf_op jit(solution)/shard_map/cond/branch_1_fun/while/body/eval_jaxpr/dot_general | solution.py:66
  126.7 3.7 %convolution_add_fusion.2 = f32[256,2048]{1,0:T(8,128)} fusion(bf16[256,480]{1,0:T(8,128)(2,1)S(1)} %reshape.119, f32[256,2048]{1,0:T(8,128)} %get-tuple-element.387, bf16[60,8,16,128]{3,2,1,0:T(8,128)(2,1)S(1)} %bitcast.90, pred[]{:T(512)S(6)} %compare.9), kind=kOutput, calls=%fused_computation.5.clone.1 | convolution fusion | flops 504365056 | bytes 6406145 | tf_op jit(solution)/shard_map/cond/branch_1_fun/while/body/eval_jaxpr/dot_general | solution.py:66
  132.0 3.7 %convolution_add_fusion.2 = f32[256,2048]{1,0:T(8,128)} fusion(bf16[256,480]{1,0:T(8,128)(2,1)S(1)} %reshape.119, f32[256,2048]{1,0:T(8,128)} %get-tuple-element.387, bf16[60,8,16,128]{3,2,1,0:T(8,128)(2,1)S(1)} %bitcast.90, pred[]{:T(512)S(6)} %compare.9), kind=kOutput, calls=%fused_computation.5.clone.1 | convolution fusion | flops 504365056 | bytes 6406145 | tf_op jit(solution)/shard_map/cond/branch_1_fun/while/body/eval_jaxpr/dot_general | solution.py:66
  136.6 0.7 convolution_convert_fusion.2
  137.4 3.7 %convolution_add_fusion.2 = f32[256,2048]{1,0:T(8,128)} fusion(bf16[256,480]{1,0:T(8,128)(2,1)S(1)} %reshape.119, f32[256,2048]{1,0:T(8,128)} %get-tuple-element.387, bf16[60,8,16,128]{3,2,1,0:T(8,128)(2,1)S(1)} %bitcast.90, pred[]{:T(512)S(6)} %compare.9), kind=kOutput, calls=%fused_computation.5.clone.1 | convolution fusion | flops 504365056 | bytes 6406145 | tf_op jit(solution)/shard_map/cond/branch_1_fun/while/body/eval_jaxpr/dot_general | solution.py:66
  141.1 2.0 %copy.92 = f32[32,8,16,128]{3,2,1,0:T(8,128)S(1)} copy(f32[32,8,16,128]{3,1,2,0:T(8,128)} %bitcast.91) | data formatting | bytes 4194304 | tf_op jit(solution)/shard_map/cond
  (134 shorter events, 18.3 us)
Async XLA Ops:
  0.0 78.2 %copy-start.1 = (bf16[8,32,128]{2,1,0:T(8,128)(2,1)S(1)}, bf16[8,32,128]{2,1,0:T(8,128)(2,1)}, u32[]{:S(2)}) copy-start(bf16[8,32,128]{2,1,0:T(8,128)(2,1)} %param.14) | copy-start | bytes 196612
  0.0 77.3 %copy-start.3 = (f32[33,33]{1,0:T(8,128)S(1)}, f32[33,33]{1,0:T(8,128)}, u32[]{:S(2)}) copy-start(f32[33,33]{1,0:T(8,128)} %param.16) | copy-start | bytes 13072
  0.0 77.3 %copy-start.4 = (s32[33,33]{1,0:T(8,128)S(1)}, s32[33,33]{1,0:T(8,128)}, u32[]{:S(2)}) copy-start(s32[33,33]{1,0:T(8,128)} %param.17) | copy-start | bytes 13072
  0.0 77.3 %copy-start = (f32[33,33]{1,0:T(8,128)S(1)}, f32[33,33]{1,0:T(8,128)}, u32[]{:S(2)}) copy-start(f32[33,33]{1,0:T(8,128)} %param.18) | copy-start | bytes 13072
  0.8 77.4 %collective-permute-start.2 = (bf16[8,16,128]{2,1,0:T(8,128)(2,1)S(1)}, bf16[8,16,128]{2,1,0:T(8,128)(2,1)S(1)}, u32[]{:S(2)}, u32[]{:S(2)}) collective-permute-start(bf16[8,16,128]{2,1,0:T(8,128)(2,1)S(1)} %get-tuple-element.298), channel_id=1, source_target_pairs={{0,2},{2,4},{4,6},{6,8},{8,10},{10,12},{12,14},{1,3},{3,5},{5,7},{... | collective-permute-start | bytes 98312 | tf_op jit(solution)/shard_map/ppermute | solution.py:17
  5.7 72.5 %collective-permute-start.3 = (bf16[8,16,128]{2,1,0:T(8,128)(2,1)S(1)}, bf16[8,16,128]{2,1,0:T(8,128)(2,1)S(1)}, u32[]{:S(2)}, u32[]{:S(2)}) collective-permute-start(bf16[8,16,128]{2,1,0:T(8,128)(2,1)S(1)} %get-tuple-element.297), channel_id=1, source_target_pairs={{2,0},{4,2},{6,4},{8,6},{10,8},{12,10},{14,12},{3,1},{5,3},{7,5},{... | collective-permute-start | bytes 98312 | tf_op jit(solution)/shard_map/ppermute | solution.py:19
  8.4 5.9 %collective-permute-start = (bf16[8,2,8]{2,0,1:T(8,128)(2,1)S(1)}, bf16[8,2,8]{2,0,1:T(8,128)(2,1)S(1)}, u32[]{:S(2)}, u32[]{:S(2)}) collective-permute-start(bf16[8,2,8]{2,0,1:T(8,128)(2,1)S(1)} %get-tuple-element.425), channel_id=1, source_target_pairs={{0,2},{2,4},{4,6},{6,8},{8,10},{10,12},{12,14},{1,3},{3,5},{5,7},{... | collective-permute-start | bytes 776 | tf_op jit(solution)/shard_map/while/body/eval_jaxpr/ppermute | solution.py:29
  12.9 5.9 %collective-permute-start.1 = (bf16[8,2,8]{2,0,1:T(8,128)(2,1)S(1)}, bf16[8,2,8]{2,0,1:T(8,128)(2,1)S(1)}, u32[]{:S(2)}, u32[]{:S(2)}) collective-permute-start(bf16[8,2,8]{2,0,1:T(8,128)(2,1)S(1)} %get-tuple-element.426), channel_id=1, source_target_pairs={{2,0},{4,2},{6,4},{8,6},{10,8},{12,10},{14,12},{3,1},{5,3},{7,5},{... | collective-permute-start | bytes 776 | tf_op jit(solution)/shard_map/while/body/eval_jaxpr/ppermute | solution.py:29
  18.9 6.1 %collective-permute-start = (bf16[8,2,8]{2,0,1:T(8,128)(2,1)S(1)}, bf16[8,2,8]{2,0,1:T(8,128)(2,1)S(1)}, u32[]{:S(2)}, u32[]{:S(2)}) collective-permute-start(bf16[8,2,8]{2,0,1:T(8,128)(2,1)S(1)} %get-tuple-element.425), channel_id=1, source_target_pairs={{0,2},{2,4},{4,6},{6,8},{8,10},{10,12},{12,14},{1,3},{3,5},{5,7},{... | collective-permute-start | bytes 776 | tf_op jit(solution)/shard_map/while/body/eval_jaxpr/ppermute | solution.py:29
  23.7 5.5 %collective-permute-start.1 = (bf16[8,2,8]{2,0,1:T(8,128)(2,1)S(1)}, bf16[8,2,8]{2,0,1:T(8,128)(2,1)S(1)}, u32[]{:S(2)}, u32[]{:S(2)}) collective-permute-start(bf16[8,2,8]{2,0,1:T(8,128)(2,1)S(1)} %get-tuple-element.426), channel_id=1, source_target_pairs={{2,0},{4,2},{6,4},{8,6},{10,8},{12,10},{14,12},{3,1},{5,3},{7,5},{... | collective-permute-start | bytes 776 | tf_op jit(solution)/shard_map/while/body/eval_jaxpr/ppermute | solution.py:29
  29.2 4.3 %collective-permute-start = (bf16[8,2,8]{2,0,1:T(8,128)(2,1)S(1)}, bf16[8,2,8]{2,0,1:T(8,128)(2,1)S(1)}, u32[]{:S(2)}, u32[]{:S(2)}) collective-permute-start(bf16[8,2,8]{2,0,1:T(8,128)(2,1)S(1)} %get-tuple-element.425), channel_id=1, source_target_pairs={{0,2},{2,4},{4,6},{6,8},{8,10},{10,12},{12,14},{1,3},{3,5},{5,7},{... | collective-permute-start | bytes 776 | tf_op jit(solution)/shard_map/while/body/eval_jaxpr/ppermute | solution.py:29
  32.2 5.5 %collective-permute-start.1 = (bf16[8,2,8]{2,0,1:T(8,128)(2,1)S(1)}, bf16[8,2,8]{2,0,1:T(8,128)(2,1)S(1)}, u32[]{:S(2)}, u32[]{:S(2)}) collective-permute-start(bf16[8,2,8]{2,0,1:T(8,128)(2,1)S(1)} %get-tuple-element.426), channel_id=1, source_target_pairs={{2,0},{4,2},{6,4},{8,6},{10,8},{12,10},{14,12},{3,1},{5,3},{7,5},{... | collective-permute-start | bytes 776 | tf_op jit(solution)/shard_map/while/body/eval_jaxpr/ppermute | solution.py:29
  37.7 6.1 %collective-permute-start = (bf16[8,2,8]{2,0,1:T(8,128)(2,1)S(1)}, bf16[8,2,8]{2,0,1:T(8,128)(2,1)S(1)}, u32[]{:S(2)}, u32[]{:S(2)}) collective-permute-start(bf16[8,2,8]{2,0,1:T(8,128)(2,1)S(1)} %get-tuple-element.425), channel_id=1, source_target_pairs={{0,2},{2,4},{4,6},{6,8},{8,10},{10,12},{12,14},{1,3},{3,5},{5,7},{... | collective-permute-start | bytes 776 | tf_op jit(solution)/shard_map/while/body/eval_jaxpr/ppermute | solution.py:29
  42.5 5.5 %collective-permute-start.1 = (bf16[8,2,8]{2,0,1:T(8,128)(2,1)S(1)}, bf16[8,2,8]{2,0,1:T(8,128)(2,1)S(1)}, u32[]{:S(2)}, u32[]{:S(2)}) collective-permute-start(bf16[8,2,8]{2,0,1:T(8,128)(2,1)S(1)} %get-tuple-element.426), channel_id=1, source_target_pairs={{2,0},{4,2},{6,4},{8,6},{10,8},{12,10},{14,12},{3,1},{5,3},{7,5},{... | collective-permute-start | bytes 776 | tf_op jit(solution)/shard_map/while/body/eval_jaxpr/ppermute | solution.py:29
  48.1 4.3 %collective-permute-start = (bf16[8,2,8]{2,0,1:T(8,128)(2,1)S(1)}, bf16[8,2,8]{2,0,1:T(8,128)(2,1)S(1)}, u32[]{:S(2)}, u32[]{:S(2)}) collective-permute-start(bf16[8,2,8]{2,0,1:T(8,128)(2,1)S(1)} %get-tuple-element.425), channel_id=1, source_target_pairs={{0,2},{2,4},{4,6},{6,8},{8,10},{10,12},{12,14},{1,3},{3,5},{5,7},{... | collective-permute-start | bytes 776 | tf_op jit(solution)/shard_map/while/body/eval_jaxpr/ppermute | solution.py:29
  51.0 5.5 %collective-permute-start.1 = (bf16[8,2,8]{2,0,1:T(8,128)(2,1)S(1)}, bf16[8,2,8]{2,0,1:T(8,128)(2,1)S(1)}, u32[]{:S(2)}, u32[]{:S(2)}) collective-permute-start(bf16[8,2,8]{2,0,1:T(8,128)(2,1)S(1)} %get-tuple-element.426), channel_id=1, source_target_pairs={{2,0},{4,2},{6,4},{8,6},{10,8},{12,10},{14,12},{3,1},{5,3},{7,5},{... | collective-permute-start | bytes 776 | tf_op jit(solution)/shard_map/while/body/eval_jaxpr/ppermute | solution.py:29
  56.5 6.1 %collective-permute-start = (bf16[8,2,8]{2,0,1:T(8,128)(2,1)S(1)}, bf16[8,2,8]{2,0,1:T(8,128)(2,1)S(1)}, u32[]{:S(2)}, u32[]{:S(2)}) collective-permute-start(bf16[8,2,8]{2,0,1:T(8,128)(2,1)S(1)} %get-tuple-element.425), channel_id=1, source_target_pairs={{0,2},{2,4},{4,6},{6,8},{8,10},{10,12},{12,14},{1,3},{3,5},{5,7},{... | collective-permute-start | bytes 776 | tf_op jit(solution)/shard_map/while/body/eval_jaxpr/ppermute | solution.py:29
  61.4 5.5 %collective-permute-start.1 = (bf16[8,2,8]{2,0,1:T(8,128)(2,1)S(1)}, bf16[8,2,8]{2,0,1:T(8,128)(2,1)S(1)}, u32[]{:S(2)}, u32[]{:S(2)}) collective-permute-start(bf16[8,2,8]{2,0,1:T(8,128)(2,1)S(1)} %get-tuple-element.426), channel_id=1, source_target_pairs={{2,0},{4,2},{6,4},{8,6},{10,8},{12,10},{14,12},{3,1},{5,3},{7,5},{... | collective-permute-start | bytes 776 | tf_op jit(solution)/shard_map/while/body/eval_jaxpr/ppermute | solution.py:29
  66.9 4.1 %collective-permute-start = (bf16[8,2,8]{2,0,1:T(8,128)(2,1)S(1)}, bf16[8,2,8]{2,0,1:T(8,128)(2,1)S(1)}, u32[]{:S(2)}, u32[]{:S(2)}) collective-permute-start(bf16[8,2,8]{2,0,1:T(8,128)(2,1)S(1)} %get-tuple-element.425), channel_id=1, source_target_pairs={{0,2},{2,4},{4,6},{6,8},{8,10},{10,12},{12,14},{1,3},{3,5},{5,7},{... | collective-permute-start | bytes 776 | tf_op jit(solution)/shard_map/while/body/eval_jaxpr/ppermute | solution.py:29
  69.7 5.5 %collective-permute-start.1 = (bf16[8,2,8]{2,0,1:T(8,128)(2,1)S(1)}, bf16[8,2,8]{2,0,1:T(8,128)(2,1)S(1)}, u32[]{:S(2)}, u32[]{:S(2)}) collective-permute-start(bf16[8,2,8]{2,0,1:T(8,128)(2,1)S(1)} %get-tuple-element.426), channel_id=1, source_target_pairs={{2,0},{4,2},{6,4},{8,6},{10,8},{12,10},{14,12},{3,1},{5,3},{7,5},{... | collective-permute-start | bytes 776 | tf_op jit(solution)/shard_map/while/body/eval_jaxpr/ppermute | solution.py:29
  75.2 8.7 %copy-start.2 = (bf16[16,32,128]{2,1,0:T(8,128)(2,1)S(1)}, bf16[16,32,128]{2,1,0:T(8,128)(2,1)}, u32[]{:S(2)}) copy-start(bf16[16,32,128]{2,1,0:T(8,128)(2,1)} %param.15) | copy-start | bytes 393220
  78.4 5.2 %collective-permute-start.4 = (bf16[8,64,16]{2,1,0:T(8,128)(2,1)S(1)}, bf16[8,64,16]{2,1,0:T(8,128)(2,1)S(1)}, u32[]{:S(2)}, u32[]{:S(2)}) collective-permute-start(bf16[8,64,16]{2,1,0:T(8,128)(2,1)S(1)} %get-tuple-element.295), channel_id=1, source_target_pairs={{0,1},{2,3},{4,5},{6,7},{8,9},{10,11},{12,13},{14,15},{16,17},{18,... | collective-permute-start | bytes 49160 | tf_op jit(solution)/shard_map/ppermute | solution.py:17
  80.5 3.2 %collective-permute-start.5 = (bf16[8,64,16]{2,1,0:T(8,128)(2,1)S(1)}, bf16[8,64,16]{2,1,0:T(8,128)(2,1)S(1)}, u32[]{:S(2)}, u32[]{:S(2)}) collective-permute-start(bf16[8,64,16]{2,1,0:T(8,128)(2,1)S(1)} %get-tuple-element.296), channel_id=1, source_target_pairs={{1,0},{3,2},{5,4},{7,6},{9,8},{11,10},{13,12},{15,14},{17,16},{19,... | collective-permute-start | bytes 49160 | tf_op jit(solution)/shard_map/ppermute | solution.py:19
where the time goes:
time: 146 us; the launch traced here: 144 us
  matrix products  47.5 us (33%)
  starting transfers between devices  46.2 us (32%)
  waiting for transfers between devices  29.8 us (20%)
  local copies, waits for them, and re-layouts  14.7 us (10%)
  other arithmetic  2.62 us (2%)
  blocking collectives  1.82 us (1%)
    dot_general x11, matrix products, add_rows(): return total + jnp.dot(shifted, banded, preferred_element_type=jnp.float32)  39.1 us
    ppermute x14, starting transfers between devices, shifted_2(): lax.ppermute(value, axis, [(source, source + steps) for source in range(l...  36.7 us
    ppermute x14, waiting for transfers between devices, shifted_2(): lax.ppermute(value, axis, [(source, source + steps) for source in range(l...  29.6 us
    dot_general x11, matrix products, add_rows(): jnp.einsum('cjd,sad->acsj', onehot, kernel_rows, preferred_element_type=j...  7.85 us
    ppermute x2, starting transfers between devices, extended_2(): lax.ppermute(tail, axis, [(i, (i + 1) % count) for i in range(ends)])  6.93 us
    another operation x22, local copies, waits for them, and re-layouts, add_rows(): jnp.stack([lax.dynamic_slice_in_dim(extended, first + k, row_count, 1) fo...  5.64 us
    reshape x11, local copies, waits for them, and re-layouts, add_rows(): shifted = shifted.reshape(band_count * row_count, group * wide_cols)  2.96 us
  transfers between devices with their start and end apart: 18, of which 8 were waited for; matrix products, arithmetic and copies ran while one was open for 3% of the time, Pallas kernels for 0%

commit v1 on v0

v1 whole, which is shorter than its diff:
```python
import functools

import jax
import jax.numpy as jnp
from jax import lax
from jax.experimental import pallas as pl
from jax.experimental.pallas import tpu as pltpu
from jax.sharding import PartitionSpec as P

DEC = 16
STEP = 16
LANES = 128
F32 = jnp.float32
BF16 = jnp.bfloat16
I32 = jnp.int32


def iota(shape, axis):
    return lax.broadcasted_iota(I32, shape, axis)


def swap(value, axes, pairs):
    return lax.ppermute(value, axes, pairs)


def shifted(value, axis, steps):
    count = lax.axis_size(axis)
    leading, last = (max(0, -steps), min(count, count - steps))
    return lax.ppermute(value, axis, [(source, source + steps) for source in range(leading, last)])


def prepare_kernel(place_ref, radiance_ref, message_ref):
    row, col = place_ref[0], place_ref[1]
    bands, rows, cols = radiance_ref.shape
    cells = radiance_ref[...].reshape(bands * rows, cols)
    place = iota((cols, 256), 0) // DEC + col * (cols // DEC)
    chooser = (iota((cols, 256), 1) // 16 == place).astype(BF16)
    sums = jnp.dot(cells, chooser, preferred_element_type=F32)
    height = rows // DEC
    own_row = (iota((bands * rows, 256), 0) % rows) // DEC + row * height
    sums = jnp.where(iota((bands * rows, 256), 1) % 16 == own_row, sums, 0.0)
    coarse = jnp.sum(sums.reshape(bands, rows, 256), axis=1) * (1.0 / (DEC * DEC))
    coarse = jnp.concatenate([coarse[:, :LANES], coarse[:, LANES:]], axis=0)
    message_ref[rows : rows + 2 * bands, :] = coarse.astype(BF16)
    lane = iota((rows, cols), 1)
    packed = jnp.zeros((rows, cols), F32)
    for b in range(bands):
        moved = pltpu.roll(radiance_ref[b].astype(F32), 16 * b, 1)
        first = 16 * b - 16 * (1 - col)
        packed = jnp.where(((lane - first) & (cols - 1)) < 16, moved, packed)
    message_ref[0:rows, :] = packed.astype(BF16)


def pack_kernel(place_ref, radiance_ref, own_ref, side_ref, first_ref, second_ref):
    row = place_ref[0]
    bands, rows, cols = radiance_ref.shape
    odd = row & 1
    near = pl.multiple_of(STEP * (1 - odd), STEP)
    away = pl.multiple_of(STEP * odd, STEP)
    first_ref[0:bands] = radiance_ref[:, pl.ds(near, STEP), :]
    first_ref[bands] = side_ref[pl.ds(near, STEP), :]
    first_ref[bands + 1] = own_ref[rows : rows + 16, :] + side_ref[rows : rows + 16, :]
    second_ref[0:bands] = radiance_ref[:, pl.ds(away, STEP), :]
    second_ref[bands] = side_ref[pl.ds(away, STEP), :]


def weights_kernel(height, place_ref, tap_ref, sector_ref, far_ref, taps_ref, spread_ref, tap_s, far_s):
    row, col = place_ref[0], place_ref[1]
    span = tap_ref.shape[0]
    tall = span + STEP - 1
    wide = taps_ref.shape[1]
    sectors = taps_ref.shape[0] // STEP
    tap_s[...] = jnp.zeros(tap_s.shape, F32)
    tap_s[0:span, 0:span] = tap_ref[...]
    tap_s[tall : tall + span, 0:span] = sector_ref[...].astype(F32)
    lane = iota((LANES, wide), 1) - tall * iota((LANES, wide), 0)
    pick = ((lane >= 0) & (lane < tall)).astype(BF16)
    both = jnp.dot(tap_s[...].astype(BF16), pick, preferred_element_type=F32)
    which = iota((tall, wide), 1) % tall == iota((tall, wide), 0)
    weight = jnp.sum(jnp.where(which, both[0:tall], 0.0), axis=0, keepdims=True)
    sector = jnp.sum(jnp.where(which, both[tall:], 0.0), axis=0, keepdims=True)
    weight = pltpu.roll(jnp.broadcast_to(weight, (STEP, wide)), 0, 1, stride=1, stride_axis=0)
    sector = pltpu.roll(jnp.broadcast_to(sector, (STEP, wide)), 0, 1, stride=1, stride_axis=0)
    for s in range(sectors):
        taps_ref[s * STEP : (s + 1) * STEP, :] = jnp.where(sector == s, weight, 0.0).astype(BF16)
    far_s[...] = jnp.zeros(far_s.shape, F32)
    far_s[8 : 8 + span, 0:span] = far_ref[...]
    reach = (span - 1) // 2
    coarse_cols = LANES // DEC
    all_cols = spread_ref.shape[0] // (2 * height)
    lane = iota((LANES, all_cols * LANES), 1)
    want = lane // LANES - coarse_cols * col - (lane % LANES) // DEC + reach
    pick = (iota((LANES, all_cols * LANES), 0) == want).astype(BF16)
    parts = []
    for i in range(2):
        start = place_ref[3] - i + 8
        whole = far_s[pl.ds(start, height), :]
        high = whole.astype(BF16)
        low = (whole - high.astype(F32)).astype(BF16)
        parts += [high.astype(F32), low.astype(F32)]
    stacked = jnp.concatenate(parts, axis=0).astype(BF16)
    moved = jnp.dot(stacked, pick, preferred_element_type=F32).astype(BF16)
    for i in range(2):
        for part in range(2):
            rows = moved[(2 * i + part) * height : (2 * i + part + 1) * height]
            for J in range(all_cols):
                at = (part * all_cols + J) * height
                spread_ref[at : at + height, i * LANES : (i + 1) * LANES] = rows[:, J * LANES : (J + 1) * LANES]


def near_kernel(place_ref, taps_ref, radiance_ref, side_ref, first_ref, second_ref, sky_ref, near_ref, tiles):
    row, col, last = place_ref[0], place_ref[1], place_ref[4]
    bands, rows, cols = radiance_ref.shape
    sectors = sky_ref.shape[0]
    span = 33
    reach = 16
    tall = STEP + span - 1
    odd = (row & 1) == 1
    keep_up = row > 0
    keep_low = row < last
    tiles[:, span * tall :, :] = jnp.zeros((2, tiles.shape[1] - span * tall, tiles.shape[2]), BF16)
    zero = jnp.zeros((STEP, cols), F32)

    def around(b, middle):
        one = first_ref[b].astype(F32)
        two = second_ref[b].astype(F32)
        up = jnp.where(keep_up, jnp.where(odd, one, two), zero)
        low = jnp.where(keep_low, jnp.where(odd, two, one), zero)
        return jnp.concatenate([up, middle.astype(F32), low], axis=0)

    packed = around(bands, side_ref[0:rows, :])
    lane = iota(packed.shape, 1)
    edge = jnp.where(col == 0, (lane < reach).astype(F32), (lane >= cols - reach).astype(F32))
    for b in range(bands):
        own = around(b, radiance_ref[b])
        aux = pltpu.roll(packed, (cols - 16 * b) % cols, 1) * edge
        slot = b % 2
        for d in range(span):
            shift = d - reach
            if shift > 0:
                value = jnp.where(lane < shift, aux, own)
            elif shift < 0:
                value = jnp.where(lane >= cols + shift, aux, own)
            else:
                value = own
            if shift:
                value = pltpu.roll(value, (cols - shift) % cols, 1)
            value = value.astype(BF16)
            for i in range(2):
                tiles[slot, d * tall : (d + 1) * tall, i * cols : (i + 1) * cols] = value[i * STEP : i * STEP + tall]
        sums = jnp.dot(taps_ref[...], tiles[slot], preferred_element_type=F32)
        for i in range(2):
            part = sums[:, i * cols : (i + 1) * cols].reshape(sectors, STEP, cols)
            sky = sky_ref[:, i * STEP : (i + 1) * STEP, :].astype(F32)
            near_ref[b, i * STEP : (i + 1) * STEP, :] = jnp.sum(part * sky, axis=0)


def finish_kernel(place_ref, spread_ref, mine_ref, theirs_ref, near_ref, out_ref):
    bands = near_ref.shape[0]
    if mine_ref.shape[0] == 2 * bands:
        known = mine_ref[...].astype(F32) + theirs_ref[...].astype(F32)
        known = jnp.concatenate([known[:bands], known[bands:]], axis=1)
    else:
        known = mine_ref[...].astype(F32)
    known = jnp.concatenate([known, known], axis=1).astype(BF16)
    far = jnp.dot(known, spread_ref[...], preferred_element_type=F32)
    land = place_ref[2] > 0
    for i in range(2):
        block = far[:, i * LANES : (i + 1) * LANES][:, None, :]
        total = near_ref[:, i * DEC : (i + 1) * DEC, :] + block
        out_ref[:, i * DEC : (i + 1) * DEC, :] = jnp.where(land, total, 0.0).astype(BF16)


def call(kernel, out_shape, operands, scratch=(), flops=0):
    in_specs = [pl.BlockSpec(memory_space=pltpu.SMEM)]
    in_specs += [pl.BlockSpec(memory_space=pltpu.VMEM)] * (len(operands) - 1)
    moved = sum(a.size * a.dtype.itemsize for a in operands)
    return pl.pallas_call(
        kernel,
        out_shape=out_shape,
        in_specs=in_specs,
        out_specs=jax.tree.map(lambda _: pl.BlockSpec(memory_space=pltpu.VMEM), out_shape),
        scratch_shapes=list(scratch),
        compiler_params=pltpu.CompilerParams(vmem_limit_bytes=40 << 20),
        cost_estimate=pl.CostEstimate(flops=flops, bytes_accessed=moved, transcendentals=0),
    )(*operands)


def coarse_window(radiance, reach):
    bands, rows, cols = radiance.shape
    coarse_rows = rows // DEC
    hops = reach // coarse_rows
    live = min(hops, lax.axis_size("row") - 1)
    blocks = radiance.astype(F32).reshape(bands, coarse_rows, DEC, cols // DEC, DEC)
    own = jnp.mean(blocks, axis=(2, 4)).astype(BF16)
    pieces = [jnp.zeros_like(own)] * (2 * hops + 1)
    pieces[hops] = own
    lower = upper = own
    for k in range(1, live + 1):
        lower = shifted(lower, "row", 1)
        upper = shifted(upper, "row", -1)
        pieces[hops - k] = lower
        pieces[hops + k] = upper
    band = jnp.concatenate(pieces, axis=1)
    band = lax.all_gather(band, "col", axis=2, tiled=True)
    return jnp.transpose(band, (0, 2, 1))


def body(radiance, sky_view, tap_weight, tap_sector, far_weight, land_mask):
    bands, rows, cols = radiance.shape
    sectors = sky_view.shape[0]
    span = tap_weight.shape[0]
    far_reach = (far_weight.shape[0] - 1) // 2
    n_row, n_col = lax.axis_size("row"), lax.axis_size("col")
    coarse_rows = rows // DEC
    compact = n_row & (n_row - 1) == 0 and n_row * coarse_rows == 16
    all_cols = n_col * cols // DEC
    row, col = lax.axis_index("row"), lax.axis_index("col")
    start = far_reach - coarse_rows * row if compact else 0 * row
    place = jnp.stack([row, col, land_mask[0, 0], start, 0 * row + n_row - 1]).astype(I32)

    def shape(*dims, kind=BF16):
        return jax.ShapeDtypeStruct(dims, kind)

    message = call(prepare_kernel, shape(rows + 16, LANES), [place, radiance])
    side = swap(message, "col", [(0, 1), (1, 0)])
    first, second = call(
        pack_kernel,
        (shape(bands + 2, STEP, LANES), shape(bands + 1, STEP, LANES)),
        [place, radiance, message, side],
    )

    def flat(r, c):
        return r * n_col + c

    def other(r, c):
        q = r + 1 if r % 2 else r - 1
        return flat(q, c) if 0 <= q < n_row else flat(r, 1 - c)

    everyone = [(r, c) for r in range(n_row) for c in range(n_col)]
    from_first = swap(first, "row", [(r, r ^ 1) for r in range(n_row)])

    height = 16 if compact else 48
    tall = span + STEP - 1
    wide = -(-span * tall // LANES) * LANES
    taps, spread = call(
        functools.partial(weights_kernel, height),
        (shape(sectors * STEP, wide), shape(2 * all_cols * height, 2 * LANES)),
        [place, tap_weight, tap_sector, far_weight],
        [pltpu.VMEM((2 * tall, LANES), F32), pltpu.VMEM((64, LANES), F32)],
        flops=10_000_000,
    )

    if compact:
        known = first[bands + 1] + from_first[bands + 1]
        known, second = lax.optimization_barrier((known, second))
        theirs = swap(known, "row", [(r, r ^ 2) for r in range(n_row)])
        from_second = swap(second, ("row", "col"), [(flat(r, c), other(r, c)) for r, c in everyone])
        step = 4
        while step < n_row:
            known = known + theirs
            theirs = swap(known, "row", [(r, r ^ step) for r in range(n_row)])
            step *= 2
    else:
        from_second = swap(second, ("row", "col"), [(flat(r, c), other(r, c)) for r, c in everyone])
        window = coarse_window(radiance, far_reach)
        window = jnp.pad(window, ((0, 0), (0, 0), (0, height - window.shape[2])))
        known = theirs = window.reshape(bands, all_cols * height)

    near = call(
        near_kernel,
        shape(bands, rows, cols, kind=F32),
        [place, taps, radiance, side, from_first, from_second, sky_view],
        [pltpu.VMEM((2, wide, 2 * cols), BF16)],
        flops=2 * sectors * STEP * wide * 2 * cols * bands,
    )
    return call(finish_kernel, shape(bands, rows, cols), [place, spread, known, theirs, near])


def solution(mesh):
    in_specs = (
        P("slab", "row", "col"),
        P("slab", "row", "col"),
        P(),
        P(),
        P(),
        P(("slab", "row"), "col"),
    )
    out_specs = P("slab", "row", "col")
    return jax.shard_map(body, mesh=mesh, in_specs=in_specs, out_specs=out_specs, check_vma=False)
```

time: 146 us -> 22.7 us (0.16)
  matrix products: 47.5 us -> 0 us
  starting transfers between devices: 46.2 us -> 9.54 us
  waiting for transfers between devices: 29.8 us -> 3.65 us
  local copies, waits for them, and re-layouts: 14.7 us -> 1.85 us
  Pallas kernels: 0 us -> 6.79 us
  other arithmetic: 2.62 us -> 0.01 us
  blocking collectives: 1.82 us -> 0 us
    dot_general x23 -> x0, matrix products: 47.5 us -> none  [the longest x11 39.1 us: add_rows(): return total + jnp.dot(shifted, banded, preferred_element_type=jnp.float32)]
    ppermute x18 -> x5, starting transfers between devices: 46.2 us -> 9.54 us  [swap(): return lax.ppermute(value, axes, pairs)]
    ppermute x18 -> x5, waiting for transfers between devices: 29.8 us -> 3.65 us  [swap(): return lax.ppermute(value, axes, pairs)]
    pallas_call x0 -> x5, Pallas kernels: none -> 6.79 us  [call(): pl.pallas_call(kernel, out_shape=out_shape, in_specs=in_specs, out_specs=...]
    another operation x24 -> x1, local copies, waits for them, and re-layouts: 5.83 us -> 0.08 us  [body(): jnp.stack([row, col, land_mask[0, 0], start, 0 * row + n_row - 1])]
    reshape x15 -> x0, local copies, waits for them, and re-layouts: 4.52 us -> none  [the longest x11 2.96 us: add_rows(): shifted = shifted.reshape(band_count * row_count, group * wide_cols)]
    cond x2 -> x0, local copies, waits for them, and re-layouts: 2.13 us -> none
    all_gather x1 -> x0, blocking collectives: 1.82 us -> none  [body(): coarse_band = lax.all_gather(coarse_band, 'col', axis=2, tiled=True)]
  transfers between devices with their start and end apart: 18 -> 5, of which waited for: 8 -> 3; matrix products, arithmetic and copies ran while one was open for 3% -> 0% of each run, Pallas kernels for 0% -> 18%
where the time goes in v1:
time: 22.7 us; the launch traced here: 22.5 us
  starting transfers between devices  9.54 us (42%)
  Pallas kernels  6.79 us (30%)
  waiting for transfers between devices  3.65 us (16%)
  local copies, waits for them, and re-layouts  1.85 us (8%)
  between operations  0.71 us (3%)
    ppermute x5, starting transfers between devices, swap(): return lax.ppermute(value, axes, pairs)  9.54 us
    pallas_call x5, Pallas kernels, call(): pl.pallas_call(kernel, out_shape=out_shape, in_specs=in_specs, out_specs=...  6.79 us
    ppermute x5, waiting for transfers between devices, swap(): return lax.ppermute(value, axes, pairs)  3.65 us
    unnamed x12, local copies, waits for them, and re-layouts  1.76 us
  transfers between devices with their start and end apart: 5, of which 3 were waited for; matrix products, arithmetic and copies ran while one was open for 0% of the time, Pallas kernels for 18%

profile of v1, /device:TPU:0, one launch (start us, length us, event | category | flops | bytes accessed | tf_op | source)
XLA Modules:
  0.0 22.5 jit_solution(1891000601410152373)
XLA Ops:
  0.7 0.1 stack.15.place_ref
  0.7 0.0 copy-start
  0.7 0.8 %copy-done = bf16[8,32,128]{2,1,0:T(8,128)(2,1)S(1)} copy-done((bf16[8,32,128]{2,1,0:T(8,128)(2,1)S(1)}, bf16[8,32,128]{2,1,0:T(8,128)(2,1)}, u32[]{:S(2)}) %copy-start) | copy-done | bytes 65560
  1.6 0.7 %shard_map.65.own_ref = bf16[48,128]{1,0:T(8,128)(2,1)S(1)} custom-call(s32[5]{0:T(128)S(1)} %stack.15.place_ref, bf16[8,32,128]{2,1,0:T(8,128)(2,1)S(1)} %copy-done), custom_call_target="tpu_custom_call" | custom-call | bytes 65556 | tf_op jit(solution)/shard_map/pallas_call | solution.py:178
  2.3 0.5 %collective-permute-start = (bf16[48,128]{1,0:T(8,128)(2,1)S(1)}, bf16[48,128]{1,0:T(8,128)(2,1)S(1)}, u32[]{:S(2)}, u32[]{:S(2)}) collective-permute-start(bf16[48,128]{1,0:T(8,128)(2,1)S(1)} %shard_map.65.own_ref), channel_id=1, source_target_pairs={{0,1},{1,0},{2,3},{3,2},{4,5},{5,4},{6,7},{7,6},{8,9},{9,8},{10,11... | collective-permute-start | bytes 36872 | tf_op jit(solution)/shard_map/ppermute | solution.py:23
  2.8 0.8 %collective-permute-done.side_ref = bf16[48,128]{1,0:T(8,128)(2,1)S(1)} collective-permute-done((bf16[48,128]{1,0:T(8,128)(2,1)S(1)}, bf16[48,128]{1,0:T(8,128)(2,1)S(1)}, u32[]{:S(2)}, u32[]{:S(2)}) %collective-permute-start) | collective-permute-done | bytes 12320 | tf_op jit(solution)/shard_map/ppermute | solution.py:23
  3.7 0.0 copy-start.2
  3.7 0.0 copy-start.3
  3.7 0.0 copy-start.4
  3.7 0.6 %shard_map.66 = (bf16[10,16,128]{2,1,0:T(8,128)(2,1)S(1)}, bf16[9,16,128]{2,1,0:T(8,128)(2,1)S(1)}) custom-call(s32[5]{0:T(128)S(1)} %stack.15.place_ref, bf16[8,32,128]{2,1,0:T(8,128)(2,1)S(1)} %copy-done, bf16[48,128]{1,0:T(8,128)(2,1)S(1)} %shard_map.65.own_ref, bf16[48,128]{1,0:T(8,128)(2,1)S(1)} %collective-permute-done.side_ref), custom_call_target="tpu_custom_call" | custom-call | bytes 90132 | tf_op jit(solution)/shard_map/pallas_call | solution.py:178
  4.2 0.0 copy-start.1
  4.2 2.9 %collective-permute-start.1 = (bf16[10,16,128]{2,1,0:T(8,128)(2,1)S(1)}, bf16[10,16,128]{2,1,0:T(8,128)(2,1)S(1)}, u32[]{:S(2)}, u32[]{:S(2)}) collective-permute-start(bf16[10,16,128]{2,1,0:T(8,128)(2,1)S(1)} %get-tuple-element.12), channel_id=1, source_target_pairs={{0,2},{2,0},{4,6},{6,4},{8,10},{10,8},{12,14},{14,12},{1,3},{3,1},... | collective-permute-start | bytes 122888 | tf_op jit(solution)/shard_map/ppermute | solution.py:23
  7.1 2.0 %collective-permute-done.1.first_ref = bf16[10,16,128]{2,1,0:T(8,128)(2,1)S(1)} collective-permute-done((bf16[10,16,128]{2,1,0:T(8,128)(2,1)S(1)}, bf16[10,16,128]{2,1,0:T(8,128)(2,1)S(1)}, u32[]{:S(2)}, u32[]{:S(2)}) %collective-permute-start.1) | collective-permute-done | bytes 40992 | tf_op jit(solution)/shard_map/ppermute | solution.py:23
  9.1 0.0 collective-permute-start.4
  9.1 3.5 %collective-permute-start.2 = (bf16[16,128]{1,0:T(8,128)(2,1)S(1)}, bf16[16,128]{1,0:T(8,128)(2,1)S(1)}, u32[]{:S(2)}, u32[]{:S(2)}) collective-permute-start(bf16[16,128]{1,0:T(8,128)(2,1)S(1)} %fusion), channel_id=1, source_target_pairs={{0,4},{2,6},{4,0},{6,2},{8,12},{10,14},{12,8},{14,10},{1,5},{3,7},... | collective-permute-start | bytes 12296 | tf_op jit(solution)/shard_map/ppermute | solution.py:23
  12.6 0.0 copy-done.2
  12.6 0.0 copy-done.3
  12.6 0.0 copy-done.4
  12.6 1.1 %shard_map.64 = (bf16[256,1664]{1,0:T(8,128)(2,1)S(1)}, bf16[512,256]{1,0:T(8,128)(2,1)S(1)}) custom-call(s32[5]{0:T(128)S(1)} %stack.15.place_ref, f32[33,33]{1,0:T(8,128)S(1)} %copy-done.2, s32[33,33]{1,0:T(8,128)S(1)} %copy-done.3, f32[33,33]{1,0:T(8,128)S(1)} %copy-done.4), custom_call_target="tpu_custom_call" | custom-call | flops 10000000 | bytes 13088 | tf_op jit(solution)/shard_map/pallas_call | solution.py:178
  13.8 0.8 %collective-permute-done.2 = bf16[16,128]{1,0:T(8,128)(2,1)S(1)} collective-permute-done((bf16[16,128]{1,0:T(8,128)(2,1)S(1)}, bf16[16,128]{1,0:T(8,128)(2,1)S(1)}, u32[]{:S(2)}, u32[]{:S(2)}) %collective-permute-start.2) | collective-permute-done | bytes 4128 | tf_op jit(solution)/shard_map/ppermute | solution.py:23
  14.6 2.6 %collective-permute-start.3 = (bf16[16,128]{1,0:T(8,128)(2,1)S(1)}, bf16[16,128]{1,0:T(8,128)(2,1)S(1)}, u32[]{:S(2)}, u32[]{:S(2)}) collective-permute-start(bf16[16,128]{1,0:T(8,128)(2,1)S(1)} %add.11.mine_ref), channel_id=1, source_target_pairs={{0,8},{2,10},{4,12},{6,14},{8,0},{10,2},{12,4},{14,6},{1,9},{3,11}... | collective-permute-start | bytes 12296 | tf_op jit(solution)/shard_map/ppermute | solution.py:23
  17.2 0.0 collective-permute-done.4.second_ref
  17.2 0.0 copy-done.1
  17.2 0.0 copy-start.5
  17.2 0.9 %copy-done.5 = bf16[16,32,128]{2,1,0:T(8,128)(2,1)S(1)} copy-done((bf16[16,32,128]{2,1,0:T(8,128)(2,1)S(1)}, bf16[16,32,128]{2,1,0:T(8,128)(2,1)}, u32[]{:S(2)}) %copy-start.5) | copy-done | bytes 131096
  18.2 3.0 %shard_map.67.near_ref = f32[8,32,128]{2,1,0:T(8,128)S(1)} custom-call(s32[5]{0:T(128)S(1)} %stack.15.place_ref, bf16[256,1664]{1,0:T(8,128)(2,1)S(1)} %get-tuple-element.15.taps_ref, bf16[8,32,128]{2,1,0:T(8,128)(2,1)S(1)} %copy-done.1, bf16[48,128]{1,0:T(8,128)(2,1)S(1)} %collective-permute-done.side_ref, ...), custom_call_target="tpu_custom_call" | custom-call | flops 1744830464 | bytes 1138708 | tf_op jit(solution)/shard_map/pallas_call | solution.py:178
  21.2 0.0 collective-permute-done.3.theirs_ref
  21.2 1.3 %shard_map.68 = bf16[8,32,128]{2,1,0:T(8,128)(2,1)} custom-call(s32[5]{0:T(128)S(1)} %stack.15.place_ref, bf16[512,256]{1,0:T(8,128)(2,1)S(1)} %get-tuple-element.11.spread_ref, bf16[16,128]{1,0:T(8,128)(2,1)S(1)} %add.11.mine_ref, bf16[16,128]{1,0:T(8,128)(2,1)S(1)} %collective-permute-done.3.theirs_ref, f32[8,32,128]{2,1,0:T(8,128)S(1)} %shard_map.67.near_ref), custom_call_target="tpu_custom_call" | custom-call | bytes 401428 | tf_op jit(solution)/shard_map/pallas_call | solution.py:178
  (2 shorter events, 0.0 us)
Async XLA Ops:
  0.7 0.8 %copy-start = (bf16[8,32,128]{2,1,0:T(8,128)(2,1)S(1)}, bf16[8,32,128]{2,1,0:T(8,128)(2,1)}, u32[]{:S(2)}) copy-start(bf16[8,32,128]{2,1,0:T(8,128)(2,1)} %radiance_ref.5) | copy-start | bytes 196612
  2.3 1.4 %collective-permute-start = (bf16[48,128]{1,0:T(8,128)(2,1)S(1)}, bf16[48,128]{1,0:T(8,128)(2,1)S(1)}, u32[]{:S(2)}, u32[]{:S(2)}) collective-permute-start(bf16[48,128]{1,0:T(8,128)(2,1)S(1)} %shard_map.65.own_ref), channel_id=1, source_target_pairs={{0,1},{1,0},{2,3},{3,2},{4,5},{5,4},{6,7},{7,6},{8,9},{9,8},{10,11... | collective-permute-start | bytes 36872 | tf_op jit(solution)/shard_map/ppermute | solution.py:23
  3.7 8.9 %copy-start.2 = (f32[33,33]{1,0:T(8,128)S(1)}, f32[33,33]{1,0:T(8,128)}, u32[]{:S(2)}) copy-start(f32[33,33]{1,0:T(8,128)} %tap_ref.1) | copy-start | bytes 13072
  3.7 8.9 %copy-start.3 = (s32[33,33]{1,0:T(8,128)S(1)}, s32[33,33]{1,0:T(8,128)}, u32[]{:S(2)}) copy-start(s32[33,33]{1,0:T(8,128)} %sector_ref.1) | copy-start | bytes 13072
  3.7 8.9 %copy-start.4 = (f32[33,33]{1,0:T(8,128)S(1)}, f32[33,33]{1,0:T(8,128)}, u32[]{:S(2)}) copy-start(f32[33,33]{1,0:T(8,128)} %far_ref.1) | copy-start | bytes 13072
  4.2 13.0 %copy-start.1 = (bf16[8,32,128]{2,1,0:T(8,128)(2,1)S(1)}, bf16[8,32,128]{2,1,0:T(8,128)(2,1)}, u32[]{:S(2)}) copy-start(bf16[8,32,128]{2,1,0:T(8,128)(2,1)} %radiance_ref.5) | copy-start | bytes 196612
  4.2 4.9 %collective-permute-start.1 = (bf16[10,16,128]{2,1,0:T(8,128)(2,1)S(1)}, bf16[10,16,128]{2,1,0:T(8,128)(2,1)S(1)}, u32[]{:S(2)}, u32[]{:S(2)}) collective-permute-start(bf16[10,16,128]{2,1,0:T(8,128)(2,1)S(1)} %get-tuple-element.12), channel_id=1, source_target_pairs={{0,2},{2,0},{4,6},{6,4},{8,10},{10,8},{12,14},{14,12},{1,3},{3,1},... | collective-permute-start | bytes 122888 | tf_op jit(solution)/shard_map/ppermute | solution.py:23
  9.1 8.1 %collective-permute-start.4 = (bf16[9,16,128]{2,1,0:T(8,128)(2,1)S(1)}, bf16[9,16,128]{2,1,0:T(8,128)(2,1)S(1)}, u32[]{:S(2)}, u32[]{:S(2)}) collective-permute-start(bf16[9,16,128]{2,1,0:T(8,128)(2,1)S(1)} %get-tuple-element.16), channel_id=1, source_target_pairs={{0,1},{1,0},{2,4},{3,5},{4,2},{5,3},{6,8},{7,9},{8,6},{9,7},{10,12... | collective-permute-start | bytes 110600 | tf_op jit(solution)/shard_map/ppermute | solution.py:23
  9.1 5.5 %collective-permute-start.2 = (bf16[16,128]{1,0:T(8,128)(2,1)S(1)}, bf16[16,128]{1,0:T(8,128)(2,1)S(1)}, u32[]{:S(2)}, u32[]{:S(2)}) collective-permute-start(bf16[16,128]{1,0:T(8,128)(2,1)S(1)} %fusion), channel_id=1, source_target_pairs={{0,4},{2,6},{4,0},{6,2},{8,12},{10,14},{12,8},{14,10},{1,5},{3,7},... | collective-permute-start | bytes 12296 | tf_op jit(solution)/shard_map/ppermute | solution.py:23
  14.6 6.6 %collective-permute-start.3 = (bf16[16,128]{1,0:T(8,128)(2,1)S(1)}, bf16[16,128]{1,0:T(8,128)(2,1)S(1)}, u32[]{:S(2)}, u32[]{:S(2)}) collective-permute-start(bf16[16,128]{1,0:T(8,128)(2,1)S(1)} %add.11.mine_ref), channel_id=1, source_target_pairs={{0,8},{2,10},{4,12},{6,14},{8,0},{10,2},{12,4},{14,6},{1,9},{3,11}... | collective-permute-start | bytes 12296 | tf_op jit(solution)/shard_map/ppermute | solution.py:23
  17.2 0.9 %copy-start.5 = (bf16[16,32,128]{2,1,0:T(8,128)(2,1)S(1)}, bf16[16,32,128]{2,1,0:T(8,128)(2,1)}, u32[]{:S(2)}) copy-start(bf16[16,32,128]{2,1,0:T(8,128)(2,1)} %sky_ref.1) | copy-start | bytes 393220

commit v2 on v1

--- a/solution.py
+++ b/solution.py
@@ -29,17 +29,17 @@
     return lax.ppermute(value, axis, [(source, source + steps) for source in range(leading, last)])
 
 
-def prepare_kernel(place_ref, radiance_ref, message_ref):
-    row, col = place_ref[0], place_ref[1]
+def prepare_kernel(radiance_ref, message_ref):
+    row, col = lax.axis_index("row"), lax.axis_index("col")
     bands, rows, cols = radiance_ref.shape
+    height = rows // DEC
     cells = radiance_ref[...].reshape(bands * rows, cols)
-    place = iota((cols, 256), 0) // DEC + col * (cols // DEC)
-    chooser = (iota((cols, 256), 1) // 16 == place).astype(BF16)
+    place = (iota((cols, 256), 0) >> 4) + col * (cols // DEC)
+    chooser = ((iota((cols, 256), 1) >> 4) == place).astype(BF16)
     sums = jnp.dot(cells, chooser, preferred_element_type=F32)
-    height = rows // DEC
-    own_row = (iota((bands * rows, 256), 0) % rows) // DEC + row * height
-    sums = jnp.where(iota((bands * rows, 256), 1) % 16 == own_row, sums, 0.0)
-    coarse = jnp.sum(sums.reshape(bands, rows, 256), axis=1) * (1.0 / (DEC * DEC))
+    sums = jnp.sum(sums.reshape(bands, height, DEC, 256), axis=2)
+    own_row = (iota((bands, height, 256), 2) & 15) - iota((bands, height, 256), 1)
+    coarse = jnp.sum(jnp.where(own_row == row * height, sums, 0.0), axis=1) * (1.0 / (DEC * DEC))
     coarse = jnp.concatenate([coarse[:, :LANES], coarse[:, LANES:]], axis=0)
     message_ref[rows : rows + 2 * bands, :] = coarse.astype(BF16)
     lane = iota((rows, cols), 1)
@@ -51,10 +51,9 @@
     message_ref[0:rows, :] = packed.astype(BF16)
 
 
-def pack_kernel(place_ref, radiance_ref, own_ref, side_ref, first_ref, second_ref):
-    row = place_ref[0]
+def pack_kernel(radiance_ref, own_ref, side_ref, first_ref, second_ref):
     bands, rows, cols = radiance_ref.shape
-    odd = row & 1
+    odd = lax.axis_index("row") & 1
     near = pl.multiple_of(STEP * (1 - odd), STEP)
     away = pl.multiple_of(STEP * odd, STEP)
     first_ref[0:bands] = radiance_ref[:, pl.ds(near, STEP), :]
@@ -64,8 +63,13 @@
     second_ref[bands] = side_ref[pl.ds(away, STEP), :]
 
 
-def weights_kernel(height, place_ref, tap_ref, sector_ref, far_ref, taps_ref, spread_ref, tap_s, far_s):
-    row, col = place_ref[0], place_ref[1]
+def weights_kernel(
+    height, whole_grid, land_ref, tap_ref, sector_ref, far_ref, sky_ref, taps_ref, spread_ref, view_ref, tap_s, far_s, sky_s, sem
+):
+    row, col = lax.axis_index("row"), lax.axis_index("col")
+    fetch = pltpu.make_async_copy(sky_ref, sky_s, sem)
+    fetch.start()
+    land = land_ref[0, 0] > 0
     span = tap_ref.shape[0]
     tall = span + STEP - 1
     wide = taps_ref.shape[1]
@@ -89,11 +93,11 @@
     coarse_cols = LANES // DEC
     all_cols = spread_ref.shape[0] // (2 * height)
     lane = iota((LANES, all_cols * LANES), 1)
-    want = lane // LANES - coarse_cols * col - (lane % LANES) // DEC + reach
-    pick = (iota((LANES, all_cols * LANES), 0) == want).astype(BF16)
+    want = (lane >> 7) - coarse_cols * col - ((lane & (LANES - 1)) >> 4) + reach
+    pick = ((iota((LANES, all_cols * LANES), 0) == want) & land).astype(BF16)
     parts = []
     for i in range(2):
-        start = place_ref[3] - i + 8
+        start = (reach - 2 * row if whole_grid else 0) - i + 8
         whole = far_s[pl.ds(start, height), :]
         high = whole.astype(BF16)
         low = (whole - high.astype(F32)).astype(BF16)
@@ -106,10 +110,12 @@
             for J in range(all_cols):
                 at = (part * all_cols + J) * height
                 spread_ref[at : at + height, i * LANES : (i + 1) * LANES] = rows[:, J * LANES : (J + 1) * LANES]
-
-
-def near_kernel(place_ref, taps_ref, radiance_ref, side_ref, first_ref, second_ref, sky_ref, near_ref, tiles):
-    row, col, last = place_ref[0], place_ref[1], place_ref[4]
+    fetch.wait()
+    view_ref[...] = jnp.where(land, sky_s[...].astype(F32), 0.0)
+
+
+def near_kernel(offset, taps_ref, radiance_ref, side_ref, first_ref, second_ref, sky_ref, near_ref, tiles):
+    row, col, last = lax.axis_index("row"), lax.axis_index("col"), lax.axis_size("row") - 1
     bands, rows, cols = radiance_ref.shape
     sectors = sky_ref.shape[0]
     span = 33
@@ -131,10 +137,11 @@
     packed = around(bands, side_ref[0:rows, :])
     lane = iota(packed.shape, 1)
     edge = jnp.where(col == 0, (lane < reach).astype(F32), (lane >= cols - reach).astype(F32))
-    for b in range(bands):
+    for n in range(near_ref.shape[0]):
+        b = offset + n
         own = around(b, radiance_ref[b])
         aux = pltpu.roll(packed, (cols - 16 * b) % cols, 1) * edge
-        slot = b % 2
+        slot = n % 2
         for d in range(span):
             shift = d - reach
             if shift > 0:
@@ -151,12 +158,13 @@
         sums = jnp.dot(taps_ref[...], tiles[slot], preferred_element_type=F32)
         for i in range(2):
             part = sums[:, i * cols : (i + 1) * cols].reshape(sectors, STEP, cols)
-            sky = sky_ref[:, i * STEP : (i + 1) * STEP, :].astype(F32)
-            near_ref[b, i * STEP : (i + 1) * STEP, :] = jnp.sum(part * sky, axis=0)
-
-
-def finish_kernel(place_ref, spread_ref, mine_ref, theirs_ref, near_ref, out_ref):
-    bands = near_ref.shape[0]
+            sky = sky_ref[:, i * STEP : (i + 1) * STEP, :]
+            near_ref[n, i * STEP : (i + 1) * STEP, :] = jnp.sum(part * sky, axis=0)
+
+
+def finish_kernel(spread_ref, mine_ref, theirs_ref, *rest):
+    near_refs, out_ref = rest[:-1], rest[-1]
+    bands = out_ref.shape[0]
     if mine_ref.shape[0] == 2 * bands:
         known = mine_ref[...].astype(F32) + theirs_ref[...].astype(F32)
         known = jnp.concatenate([known[:bands], known[bands:]], axis=1)
@@ -164,22 +172,28 @@
         known = mine_ref[...].astype(F32)
     known = jnp.concatenate([known, known], axis=1).astype(BF16)
     far = jnp.dot(known, spread_ref[...], preferred_element_type=F32)
-    land = place_ref[2] > 0
-    for i in range(2):
-        block = far[:, i * LANES : (i + 1) * LANES][:, None, :]
-        total = near_ref[:, i * DEC : (i + 1) * DEC, :] + block
-        out_ref[:, i * DEC : (i + 1) * DEC, :] = jnp.where(land, total, 0.0).astype(BF16)
-
-
-def call(kernel, out_shape, operands, scratch=(), flops=0):
-    in_specs = [pl.BlockSpec(memory_space=pltpu.SMEM)]
-    in_specs += [pl.BlockSpec(memory_space=pltpu.VMEM)] * (len(operands) - 1)
+    at = 0
+    for near_ref in near_refs:
+        count = near_ref.shape[0]
+        for i in range(2):
+            block = far[at : at + count, i * LANES : (i + 1) * LANES][:, None, :]
+            total = near_ref[:, i * DEC : (i + 1) * DEC, :] + block
+            out_ref[at : at + count, i * DEC : (i + 1) * DEC, :] = total.astype(BF16)
+        at += count
+
+
+VMEM = pl.BlockSpec(memory_space=pltpu.VMEM)
+SMEM = pl.BlockSpec(memory_space=pltpu.SMEM)
+HBM = pl.BlockSpec(memory_space=pl.ANY)
+
+
+def call(kernel, out_shape, operands, scratch=(), flops=0, in_specs=None):
     moved = sum(a.size * a.dtype.itemsize for a in operands)
     return pl.pallas_call(
         kernel,
         out_shape=out_shape,
-        in_specs=in_specs,
-        out_specs=jax.tree.map(lambda _: pl.BlockSpec(memory_space=pltpu.VMEM), out_shape),
+        in_specs=in_specs or [VMEM] * len(operands),
+        out_specs=jax.tree.map(lambda _: VMEM, out_shape),
         scratch_shapes=list(scratch),
         compiler_params=pltpu.CompilerParams(vmem_limit_bytes=40 << 20),
         cost_estimate=pl.CostEstimate(flops=flops, bytes_accessed=moved, transcendentals=0),
@@ -215,19 +229,16 @@
     coarse_rows = rows // DEC
     compact = n_row & (n_row - 1) == 0 and n_row * coarse_rows == 16
     all_cols = n_col * cols // DEC
-    row, col = lax.axis_index("row"), lax.axis_index("col")
-    start = far_reach - coarse_rows * row if compact else 0 * row
-    place = jnp.stack([row, col, land_mask[0, 0], start, 0 * row + n_row - 1]).astype(I32)
 
     def shape(*dims, kind=BF16):
         return jax.ShapeDtypeStruct(dims, kind)
 
-    message = call(prepare_kernel, shape(rows + 16, LANES), [place, radiance])
+    message = call(prepare_kernel, shape(rows + 16, LANES), [radiance])
     side = swap(message, "col", [(0, 1), (1, 0)])
     first, second = call(
         pack_kernel,
         (shape(bands + 2, STEP, LANES), shape(bands + 1, STEP, LANES)),
-        [place, radiance, message, side],
+        [radiance, message, side],
     )
 
     def flat(r, c):
@@ -239,42 +250,53 @@
 
     everyone = [(r, c) for r in range(n_row) for c in range(n_col)]
     from_first = swap(first, "row", [(r, r ^ 1) for r in range(n_row)])
+    from_second = swap(second, ("row", "col"), [(flat(r, c), other(r, c)) for r, c in everyone])
 
     height = 16 if compact else 48
     tall = span + STEP - 1
     wide = -(-span * tall // LANES) * LANES
-    taps, spread = call(
-        functools.partial(weights_kernel, height),
-        (shape(sectors * STEP, wide), shape(2 * all_cols * height, 2 * LANES)),
-        [place, tap_weight, tap_sector, far_weight],
-        [pltpu.VMEM((2 * tall, LANES), F32), pltpu.VMEM((64, LANES), F32)],
+    taps, spread, sky = call(
+        functools.partial(weights_kernel, height, compact),
+        (shape(sectors * STEP, wide), shape(2 * all_cols * height, 2 * LANES), shape(sectors, rows, cols, kind=F32)),
+        [land_mask, tap_weight, tap_sector, far_weight, sky_view],
+        [
+            pltpu.VMEM((2 * tall, LANES), F32),
+            pltpu.VMEM((64, LANES), F32),
+            pltpu.VMEM(sky_view.shape, BF16),
+            pltpu.SemaphoreType.DMA,
+        ],
+        in_specs=[SMEM, VMEM, VMEM, VMEM, HBM],
         flops=10_000_000,
     )
 
+    def near(at, count):
+        return call(
+            functools.partial(near_kernel, at),
+            shape(count, rows, cols, kind=F32),
+            [taps, radiance, side, from_first, from_second, sky],
+            [pltpu.VMEM((2, wide, 2 * cols), BF16)],
+            flops=2 * sectors * STEP * wide * 2 * cols * count,
+        )
+
+    half = bands // 2
     if compact:
+        from_first, taps, spread, sky = lax.optimization_barrier((from_first, taps, spread, sky))
         known = first[bands + 1] + from_first[bands + 1]
-        known, second = lax.optimization_barrier((known, second))
         theirs = swap(known, "row", [(r, r ^ 2) for r in range(n_row)])
-        from_second = swap(second, ("row", "col"), [(flat(r, c), other(r, c)) for r, c in everyone])
+        near_one = near(0, half)
+        theirs, near_one = lax.optimization_barrier((theirs, near_one))
         step = 4
         while step < n_row:
             known = known + theirs
             theirs = swap(known, "row", [(r, r ^ step) for r in range(n_row)])
             step *= 2
     else:
-        from_second = swap(second, ("row", "col"), [(flat(r, c), other(r, c)) for r, c in everyone])
+        near_one = near(0, half)
         window = coarse_window(radiance, far_reach)
         window = jnp.pad(window, ((0, 0), (0, 0), (0, height - window.shape[2])))
         known = theirs = window.reshape(bands, all_cols * height)
-
-    near = call(
-        near_kernel,
-        shape(bands, rows, cols, kind=F32),
-        [place, taps, radiance, side, from_first, from_second, sky_view],
-        [pltpu.VMEM((2, wide, 2 * cols), BF16)],
-        flops=2 * sectors * STEP * wide * 2 * cols * bands,
-    )
-    return call(finish_kernel, shape(bands, rows, cols), [place, spread, known, theirs, near])
+    near_two = near(half, bands - half)
+    return call(finish_kernel, shape(bands, rows, cols), [spread, known, theirs, near_one, near_two])
 
 
 def solution(mesh):

time: 22.7 us -> 19.9 us (0.88)
  Pallas kernels: 6.79 us -> 4.52 us
  waiting for transfers between devices: 3.65 us -> 1.71 us
  starting transfers between devices: 9.54 us -> 10.3 us
  local copies, waits for them, and re-layouts: 1.85 us -> 2.3 us
    pallas_call x5 -> x6, Pallas kernels: 6.79 us -> 4.52 us  [call(): pl.pallas_call(kernel, out_shape=out_shape, in_specs=in_specs or [VMEM] *...]
    ppermute x5, waiting for transfers between devices: 3.65 us -> 1.71 us  [swap(): return lax.ppermute(value, axes, pairs)]
    ppermute x5, starting transfers between devices: 9.54 us -> 10.3 us  [swap(): return lax.ppermute(value, axes, pairs)]
    unnamed x12, local copies, waits for them, and re-layouts: 1.76 us -> 2.3 us
where the time goes in v2:
time: 19.9 us; the launch traced here: 19.6 us
  starting transfers between devices  10.3 us (52%)
  Pallas kernels  4.52 us (23%)
  local copies, waits for them, and re-layouts  2.3 us (12%)
  waiting for transfers between devices  1.71 us (9%)
  between operations  0.75 us (4%)
    ppermute x5, starting transfers between devices, swap(): return lax.ppermute(value, axes, pairs)  10.3 us
    pallas_call x6, Pallas kernels, call(): pl.pallas_call(kernel, out_shape=out_shape, in_specs=in_specs or [VMEM] *...  4.52 us
    unnamed x12, local copies, waits for them, and re-layouts  2.3 us
    ppermute x5, waiting for transfers between devices, swap(): return lax.ppermute(value, axes, pairs)  1.71 us
  transfers between devices with their start and end apart: 5, of which 3 were waited for; matrix products, arithmetic and copies ran while one was open for 0% of the time, Pallas kernels for 18%

profile of v2, /device:TPU:0, one launch (start us, length us, event | category | flops | bytes accessed | tf_op | source)
XLA Modules:
  0.0 19.6 jit_solution(14649511588650962195)
XLA Ops:
  0.0 0.0 copy-start
  0.0 0.8 %copy-done = bf16[8,32,128]{2,1,0:T(8,128)(2,1)S(1)} copy-done((bf16[8,32,128]{2,1,0:T(8,128)(2,1)S(1)}, bf16[8,32,128]{2,1,0:T(8,128)(2,1)}, u32[]{:S(2)}) %copy-start) | copy-done | bytes 65560
  0.8 0.0 copy-start.2
  0.8 0.2 %shard_map.64.own_ref = bf16[48,128]{1,0:T(8,128)(2,1)S(1)} custom-call(bf16[8,32,128]{2,1,0:T(8,128)(2,1)S(1)} %copy-done), custom_call_target="tpu_custom_call" | custom-call | bytes 65536 | tf_op jit(solution)/shard_map/pallas_call | solution.py:192
  1.1 0.0 copy-start.3
  1.1 0.5 %collective-permute-start = (bf16[48,128]{1,0:T(8,128)(2,1)S(1)}, bf16[48,128]{1,0:T(8,128)(2,1)S(1)}, u32[]{:S(2)}, u32[]{:S(2)}) collective-permute-start(bf16[48,128]{1,0:T(8,128)(2,1)S(1)} %shard_map.64.own_ref), channel_id=1, source_target_pairs={{0,1},{1,0},{2,3},{3,2},{4,5},{5,4},{6,7},{7,6},{8,9},{9,8},{10,11... | collective-permute-start | bytes 36872 | tf_op jit(solution)/shard_map/ppermute | solution.py:23
  1.6 0.8 %collective-permute-done.side_ref = bf16[48,128]{1,0:T(8,128)(2,1)S(1)} collective-permute-done((bf16[48,128]{1,0:T(8,128)(2,1)S(1)}, bf16[48,128]{1,0:T(8,128)(2,1)S(1)}, u32[]{:S(2)}, u32[]{:S(2)}) %collective-permute-start) | collective-permute-done | bytes 12320 | tf_op jit(solution)/shard_map/ppermute | solution.py:23
  2.4 2.9 %collective-permute-start.1 = (bf16[10,16,128]{2,1,0:T(8,128)(2,1)S(1)}, bf16[10,16,128]{2,1,0:T(8,128)(2,1)S(1)}, u32[]{:S(2)}, u32[]{:S(2)}) collective-permute-start(bf16[10,16,128]{2,1,0:T(8,128)(2,1)S(1)} %get-tuple-element.16), channel_id=1, source_target_pairs={{0,2},{2,0},{4,6},{6,4},{8,10},{10,8},{12,14},{14,12},{1,3},{3,1},... | collective-permute-start | bytes 122888 | tf_op jit(solution)/shard_map/ppermute | solution.py:23
  6.0 0.0 copy-done.2
  6.0 0.0 copy-done.3
  6.0 0.0 copy-start.4
  6.0 0.7 %copy-done.4 = s32[33,33]{1,0:T(8,128)S(1)} copy-done((s32[33,33]{1,0:T(8,128)S(1)}, s32[33,33]{1,0:T(8,128)}, u32[]{:S(2)}) %copy-start.4) | copy-done | bytes 4380
  6.7 0.0 copy-start.5
  6.7 0.7 %copy-done.5 = f32[33,33]{1,0:T(8,128)S(1)} copy-done((f32[33,33]{1,0:T(8,128)S(1)}, f32[33,33]{1,0:T(8,128)}, u32[]{:S(2)}) %copy-start.5) | copy-done | bytes 4380
  7.5 0.0 copy-start.1
  7.5 0.8 %shard_map.66 = (bf16[256,1664]{1,0:T(8,128)(2,1)S(1)}, bf16[512,256]{1,0:T(8,128)(2,1)S(1)}, f32[16,32,128]{2,1,0:T(8,128)S(1)}) custom-call(s32[1,1]{1,0:T(1,128)S(6)} %copy.7.land_ref, f32[33,33]{1,0:T(8,128)S(1)} %copy-done.3, s32[33,33]{1,0:T(8,128)S(1)} %copy-done.4, f32[33,33]{1,0:T(8,128)S(1)} %copy-done.5, bf16[16,32,128]{2,1,0:T(8,128)(2,1)S(1)} %copy-done.2), custom_call_target="tpu_custom_call" | custom-call | flops 10000000 | bytes 144144 | tf_op jit(solution)/shard_map/pallas_call | solution.py:192
  8.2 0.1 collective-permute-start.3
  8.3 0.0 collective-permute-done.1.first_ref
  8.4 1.6 %collective-permute-start.2 = (bf16[16,128]{1,0:T(8,128)(2,1)S(1)}, bf16[16,128]{1,0:T(8,128)(2,1)S(1)}, u32[]{:S(2)}, u32[]{:S(2)}) collective-permute-start(bf16[16,128]{1,0:T(8,128)(2,1)S(1)} %add_bitcast_fusion), channel_id=1, source_target_pairs={{0,4},{2,6},{4,0},{6,2},{8,12},{10,14},{12,8},{14,10},{1,5},{3,7},... | collective-permute-start | bytes 12296 | tf_op jit(solution)/shard_map/ppermute | solution.py:23
  10.0 0.0 collective-permute-done.3.second_ref
  10.0 0.0 copy-done.1
  10.0 1.4 %shard_map.67.rest_0_ = f32[4,32,128]{2,1,0:T(8,128)S(1)} custom-call(bf16[256,1664]{1,0:T(8,128)(2,1)S(1)} %get-tuple-element.22.taps_ref, bf16[8,32,128]{2,1,0:T(8,128)(2,1)S(1)} %copy-done.1, bf16[48,128]{1,0:T(8,128)(2,1)S(1)} %collective-permute-done.side_ref, bf16[10,16,128]{2,1,0:T(8,128)(2,1)S(1)} %collective-permute-done.1.first_ref, ...), custom_call_target="tpu_custom_call" | custom-call | flops 872415232 | bytes 1269760 | tf_op jit(solution)/shard_map/pallas_call | solution.py:192
  11.4 0.7 %collective-permute-done.2 = bf16[16,128]{1,0:T(8,128)(2,1)S(1)} collective-permute-done((bf16[16,128]{1,0:T(8,128)(2,1)S(1)}, bf16[16,128]{1,0:T(8,128)(2,1)S(1)}, u32[]{:S(2)}, u32[]{:S(2)}) %collective-permute-start.2) | collective-permute-done | bytes 4128 | tf_op jit(solution)/shard_map/ppermute | solution.py:23
  12.0 5.2 %collective-permute-start.4 = (bf16[16,128]{1,0:T(8,128)(2,1)S(1)}, bf16[16,128]{1,0:T(8,128)(2,1)S(1)}, u32[]{:S(2)}, u32[]{:S(2)}) collective-permute-start(bf16[16,128]{1,0:T(8,128)(2,1)S(1)} %add.11.mine_ref), channel_id=1, source_target_pairs={{0,8},{2,10},{4,12},{6,14},{8,0},{10,2},{12,4},{14,6},{1,9},{3,11}... | collective-permute-start | bytes 12296 | tf_op jit(solution)/shard_map/ppermute | solution.py:23
  17.2 1.4 %shard_map.68.rest_1_ = f32[4,32,128]{2,1,0:T(8,128)S(1)} custom-call(bf16[256,1664]{1,0:T(8,128)(2,1)S(1)} %get-tuple-element.22.taps_ref, bf16[8,32,128]{2,1,0:T(8,128)(2,1)S(1)} %copy-done.1, bf16[48,128]{1,0:T(8,128)(2,1)S(1)} %collective-permute-done.side_ref, bf16[10,16,128]{2,1,0:T(8,128)(2,1)S(1)} %collective-permute-done.1.first_ref, ...), custom_call_target="tpu_custom_call" | custom-call | flops 872415232 | bytes 1269760 | tf_op jit(solution)/shard_map/pallas_call | solution.py:192
  18.6 0.2 %collective-permute-done.4.theirs_ref = bf16[16,128]{1,0:T(8,128)(2,1)S(1)} collective-permute-done((bf16[16,128]{1,0:T(8,128)(2,1)S(1)}, bf16[16,128]{1,0:T(8,128)(2,1)S(1)}, u32[]{:S(2)}, u32[]{:S(2)}) %collective-permute-start.4) | collective-permute-done | bytes 4128 | tf_op jit(solution)/shard_map/ppermute | solution.py:23
  18.8 0.8 %shard_map.69 = bf16[8,32,128]{2,1,0:T(8,128)(2,1)} custom-call(bf16[512,256]{1,0:T(8,128)(2,1)S(1)} %get-tuple-element.20.spread_ref, bf16[16,128]{1,0:T(8,128)(2,1)S(1)} %add.11.mine_ref, bf16[16,128]{1,0:T(8,128)(2,1)S(1)} %collective-permute-done.4.theirs_ref, f32[4,32,128]{2,1,0:T(8,128)S(1)} %shard_map.67.rest_0_, f32[4,32,128]{2,1,0:T(8,128)S(1)} %shard_map.68.rest_1_), custom_call_target="tpu_custom_call" | custom-call | bytes 401408 | tf_op jit(solution)/shard_map/pallas_call | solution.py:192
  (3 shorter events, 0.0 us)
Async XLA Ops:
  0.0 0.8 %copy-start = (bf16[8,32,128]{2,1,0:T(8,128)(2,1)S(1)}, bf16[8,32,128]{2,1,0:T(8,128)(2,1)}, u32[]{:S(2)}) copy-start(bf16[8,32,128]{2,1,0:T(8,128)(2,1)} %radiance_ref.7) | copy-start | bytes 196612
  0.8 5.1 %copy-start.2 = (bf16[16,32,128]{2,1,0:T(8,128)(2,1)S(1)}, bf16[16,32,128]{2,1,0:T(8,128)(2,1)}, u32[]{:S(2)}) copy-start(bf16[16,32,128]{2,1,0:T(8,128)(2,1)} %sky_ref.1) | copy-start | bytes 393220
  1.1 4.9 %copy-start.3 = (f32[33,33]{1,0:T(8,128)S(1)}, f32[33,33]{1,0:T(8,128)}, u32[]{:S(2)}) copy-start(f32[33,33]{1,0:T(8,128)} %tap_ref.1) | copy-start | bytes 13072
  1.1 1.4 %collective-permute-start = (bf16[48,128]{1,0:T(8,128)(2,1)S(1)}, bf16[48,128]{1,0:T(8,128)(2,1)S(1)}, u32[]{:S(2)}, u32[]{:S(2)}) collective-permute-start(bf16[48,128]{1,0:T(8,128)(2,1)S(1)} %shard_map.64.own_ref), channel_id=1, source_target_pairs={{0,1},{1,0},{2,3},{3,2},{4,5},{5,4},{6,7},{7,6},{8,9},{9,8},{10,11... | collective-permute-start | bytes 36872 | tf_op jit(solution)/shard_map/ppermute | solution.py:23
  2.4 5.9 %collective-permute-start.1 = (bf16[10,16,128]{2,1,0:T(8,128)(2,1)S(1)}, bf16[10,16,128]{2,1,0:T(8,128)(2,1)S(1)}, u32[]{:S(2)}, u32[]{:S(2)}) collective-permute-start(bf16[10,16,128]{2,1,0:T(8,128)(2,1)S(1)} %get-tuple-element.16), channel_id=1, source_target_pairs={{0,2},{2,0},{4,6},{6,4},{8,10},{10,8},{12,14},{14,12},{1,3},{3,1},... | collective-permute-start | bytes 122888 | tf_op jit(solution)/shard_map/ppermute | solution.py:23
  6.0 0.7 %copy-start.4 = (s32[33,33]{1,0:T(8,128)S(1)}, s32[33,33]{1,0:T(8,128)}, u32[]{:S(2)}) copy-start(s32[33,33]{1,0:T(8,128)} %sector_ref.1) | copy-start | bytes 13072
  6.7 0.7 %copy-start.5 = (f32[33,33]{1,0:T(8,128)S(1)}, f32[33,33]{1,0:T(8,128)}, u32[]{:S(2)}) copy-start(f32[33,33]{1,0:T(8,128)} %far_ref.1) | copy-start | bytes 13072
  7.5 2.5 %copy-start.1 = (bf16[8,32,128]{2,1,0:T(8,128)(2,1)S(1)}, bf16[8,32,128]{2,1,0:T(8,128)(2,1)}, u32[]{:S(2)}) copy-start(bf16[8,32,128]{2,1,0:T(8,128)(2,1)} %radiance_ref.7) | copy-start | bytes 196612
  8.2 1.7 %collective-permute-start.3 = (bf16[9,16,128]{2,1,0:T(8,128)(2,1)S(1)}, bf16[9,16,128]{2,1,0:T(8,128)(2,1)S(1)}, u32[]{:S(2)}, u32[]{:S(2)}) collective-permute-start(bf16[9,16,128]{2,1,0:T(8,128)(2,1)S(1)} %get-tuple-element.23), channel_id=1, source_target_pairs={{0,1},{1,0},{2,4},{3,5},{4,2},{5,3},{6,8},{7,9},{8,6},{9,7},{10,12... | collective-permute-start | bytes 110600 | tf_op jit(solution)/shard_map/ppermute | solution.py:23
  8.4 3.7 %collective-permute-start.2 = (bf16[16,128]{1,0:T(8,128)(2,1)S(1)}, bf16[16,128]{1,0:T(8,128)(2,1)S(1)}, u32[]{:S(2)}, u32[]{:S(2)}) collective-permute-start(bf16[16,128]{1,0:T(8,128)(2,1)S(1)} %add_bitcast_fusion), channel_id=1, source_target_pairs={{0,4},{2,6},{4,0},{6,2},{8,12},{10,14},{12,8},{14,10},{1,5},{3,7},... | collective-permute-start | bytes 12296 | tf_op jit(solution)/shard_map/ppermute | solution.py:23
  12.0 6.8 %collective-permute-start.4 = (bf16[16,128]{1,0:T(8,128)(2,1)S(1)}, bf16[16,128]{1,0:T(8,128)(2,1)S(1)}, u32[]{:S(2)}, u32[]{:S(2)}) collective-permute-start(bf16[16,128]{1,0:T(8,128)(2,1)S(1)} %add.11.mine_ref), channel_id=1, source_target_pairs={{0,8},{2,10},{4,12},{6,14},{8,0},{10,2},{12,4},{14,6},{1,9},{3,11}... | collective-permute-start | bytes 12296 | tf_op jit(solution)/shard_map/ppermute | solution.py:23

commit v3 on v2

--- a/solution.py
+++ b/solution.py
@@ -29,9 +29,14 @@
     return lax.ppermute(value, axis, [(source, source + steps) for source in range(leading, last)])
 
 
-def prepare_kernel(radiance_ref, message_ref):
+def prepare_kernel(radiance, tap, sector, far, message_ref, radiance_ref, tap_ref, sector_ref, far_ref, sems):
+    pairs = [(radiance, radiance_ref), (tap, tap_ref), (sector, sector_ref), (far, far_ref)]
+    fetches = [pltpu.make_async_copy(*pair, sems.at[k]) for k, pair in enumerate(pairs)]
+    for fetch in fetches:
+        fetch.start()
     row, col = lax.axis_index("row"), lax.axis_index("col")
     bands, rows, cols = radiance_ref.shape
+    fetches[0].wait()
     height = rows // DEC
     cells = radiance_ref[...].reshape(bands * rows, cols)
     place = (iota((cols, 256), 0) >> 4) + col * (cols // DEC)
@@ -49,9 +54,11 @@
         first = 16 * b - 16 * (1 - col)
         packed = jnp.where(((lane - first) & (cols - 1)) < 16, moved, packed)
     message_ref[0:rows, :] = packed.astype(BF16)
-
-
-def pack_kernel(radiance_ref, own_ref, side_ref, first_ref, second_ref):
+    for fetch in fetches[1:]:
+        fetch.wait()
+
+
+def pack_kernel(land_ref, radiance_ref, own_ref, side_ref, first_ref, second_ref, keep_ref):
     bands, rows, cols = radiance_ref.shape
     odd = lax.axis_index("row") & 1
     near = pl.multiple_of(STEP * (1 - odd), STEP)
@@ -61,15 +68,14 @@
     first_ref[bands + 1] = own_ref[rows : rows + 16, :] + side_ref[rows : rows + 16, :]
     second_ref[0:bands] = radiance_ref[:, pl.ds(away, STEP), :]
     second_ref[bands] = side_ref[pl.ds(away, STEP), :]
+    ones = jnp.ones(keep_ref.shape, F32)
+    keep_ref[...] = jnp.where(land_ref[0, 0] > 0, ones, jnp.zeros_like(ones))
 
 
 def weights_kernel(
-    height, whole_grid, land_ref, tap_ref, sector_ref, far_ref, sky_ref, taps_ref, spread_ref, view_ref, tap_s, far_s, sky_s, sem
+    height, whole_grid, tap_ref, sector_ref, far_ref, sky_ref, taps_ref, spread_ref, view_ref, tap_s, far_s
 ):
     row, col = lax.axis_index("row"), lax.axis_index("col")
-    fetch = pltpu.make_async_copy(sky_ref, sky_s, sem)
-    fetch.start()
-    land = land_ref[0, 0] > 0
     span = tap_ref.shape[0]
     tall = span + STEP - 1
     wide = taps_ref.shape[1]
@@ -94,7 +100,7 @@
     all_cols = spread_ref.shape[0] // (2 * height)
     lane = iota((LANES, all_cols * LANES), 1)
     want = (lane >> 7) - coarse_cols * col - ((lane & (LANES - 1)) >> 4) + reach
-    pick = ((iota((LANES, all_cols * LANES), 0) == want) & land).astype(BF16)
+    pick = (iota((LANES, all_cols * LANES), 0) == want).astype(BF16)
     parts = []
     for i in range(2):
         start = (reach - 2 * row if whole_grid else 0) - i + 8
@@ -110,8 +116,7 @@
             for J in range(all_cols):
                 at = (part * all_cols + J) * height
                 spread_ref[at : at + height, i * LANES : (i + 1) * LANES] = rows[:, J * LANES : (J + 1) * LANES]
-    fetch.wait()
-    view_ref[...] = jnp.where(land, sky_s[...].astype(F32), 0.0)
+    view_ref[...] = sky_ref[...].astype(F32)
 
 
 def near_kernel(offset, taps_ref, radiance_ref, side_ref, first_ref, second_ref, sky_ref, near_ref, tiles):
@@ -162,9 +167,10 @@
             near_ref[n, i * STEP : (i + 1) * STEP, :] = jnp.sum(part * sky, axis=0)
 
 
-def finish_kernel(spread_ref, mine_ref, theirs_ref, *rest):
+def finish_kernel(keep_ref, spread_ref, mine_ref, theirs_ref, *rest):
     near_refs, out_ref = rest[:-1], rest[-1]
     bands = out_ref.shape[0]
+    land = keep_ref[0:1, :] > 0
     if mine_ref.shape[0] == 2 * bands:
         known = mine_ref[...].astype(F32) + theirs_ref[...].astype(F32)
         known = jnp.concatenate([known[:bands], known[bands:]], axis=1)
@@ -178,16 +184,16 @@
         for i in range(2):
             block = far[at : at + count, i * LANES : (i + 1) * LANES][:, None, :]
             total = near_ref[:, i * DEC : (i + 1) * DEC, :] + block
-            out_ref[at : at + count, i * DEC : (i + 1) * DEC, :] = total.astype(BF16)
+            out_ref[at : at + count, i * DEC : (i + 1) * DEC, :] = jnp.where(land, total, 0.0).astype(BF16)
         at += count
 
 
 VMEM = pl.BlockSpec(memory_space=pltpu.VMEM)
 SMEM = pl.BlockSpec(memory_space=pltpu.SMEM)
-HBM = pl.BlockSpec(memory_space=pl.ANY)
-
-
-def call(kernel, out_shape, operands, scratch=(), flops=0, in_specs=None):
+HBM = pl.BlockSpec(memory_space=pltpu.HBM)
+
+
+def call(kernel, out_shape, operands, scratch=(), flops=0, in_specs=None, vmem=40 << 20):
     moved = sum(a.size * a.dtype.itemsize for a in operands)
     return pl.pallas_call(
         kernel,
@@ -195,7 +201,7 @@
         in_specs=in_specs or [VMEM] * len(operands),
         out_specs=jax.tree.map(lambda _: VMEM, out_shape),
         scratch_shapes=list(scratch),
-        compiler_params=pltpu.CompilerParams(vmem_limit_bytes=40 << 20),
+        compiler_params=pltpu.CompilerParams(vmem_limit_bytes=vmem),
         cost_estimate=pl.CostEstimate(flops=flops, bytes_accessed=moved, transcendentals=0),
     )(*operands)
 
@@ -233,12 +239,20 @@
     def shape(*dims, kind=BF16):
         return jax.ShapeDtypeStruct(dims, kind)
 
-    message = call(prepare_kernel, shape(rows + 16, LANES), [radiance])
+    inputs = [radiance, tap_weight, tap_sector, far_weight]
+    message, radiance, tap_weight, tap_sector, far_weight = call(
+        prepare_kernel,
+        [shape(rows + 16, LANES)] + [jax.ShapeDtypeStruct(a.shape, a.dtype) for a in inputs],
+        [pltpu.with_memory_space_constraint(a, pltpu.HBM) for a in inputs],
+        [pltpu.SemaphoreType.DMA((len(inputs),))],
+        in_specs=[HBM] * len(inputs),
+    )
     side = swap(message, "col", [(0, 1), (1, 0)])
-    first, second = call(
+    first, second, keep = call(
         pack_kernel,
-        (shape(bands + 2, STEP, LANES), shape(bands + 1, STEP, LANES)),
-        [radiance, message, side],
+        (shape(bands + 2, STEP, LANES), shape(bands + 1, STEP, LANES), shape(8, LANES, kind=F32)),
+        [land_mask, radiance, message, side],
+        in_specs=[SMEM] + [VMEM] * 3,
     )
 
     def flat(r, c):
@@ -252,23 +266,17 @@
     from_first = swap(first, "row", [(r, r ^ 1) for r in range(n_row)])
     from_second = swap(second, ("row", "col"), [(flat(r, c), other(r, c)) for r, c in everyone])
 
+    from_first, tap_weight = lax.optimization_barrier((from_first, tap_weight))
     height = 16 if compact else 48
     tall = span + STEP - 1
     wide = -(-span * tall // LANES) * LANES
     taps, spread, sky = call(
         functools.partial(weights_kernel, height, compact),
         (shape(sectors * STEP, wide), shape(2 * all_cols * height, 2 * LANES), shape(sectors, rows, cols, kind=F32)),
-        [land_mask, tap_weight, tap_sector, far_weight, sky_view],
-        [
-            pltpu.VMEM((2 * tall, LANES), F32),
-            pltpu.VMEM((64, LANES), F32),
-            pltpu.VMEM(sky_view.shape, BF16),
-            pltpu.SemaphoreType.DMA,
-        ],
-        in_specs=[SMEM, VMEM, VMEM, VMEM, HBM],
+        [tap_weight, tap_sector, far_weight, sky_view],
+        [pltpu.VMEM((2 * tall, LANES), F32), pltpu.VMEM((64, LANES), F32)],
         flops=10_000_000,
     )
-
     def near(at, count):
         return call(
             functools.partial(near_kernel, at),
@@ -280,7 +288,6 @@
 
     half = bands // 2
     if compact:
-        from_first, taps, spread, sky = lax.optimization_barrier((from_first, taps, spread, sky))
         known = first[bands + 1] + from_first[bands + 1]
         theirs = swap(known, "row", [(r, r ^ 2) for r in range(n_row)])
         near_one = near(0, half)
@@ -296,7 +303,7 @@
         window = jnp.pad(window, ((0, 0), (0, 0), (0, height - window.shape[2])))
         known = theirs = window.reshape(bands, all_cols * height)
     near_two = near(half, bands - half)
-    return call(finish_kernel, shape(bands, rows, cols), [spread, known, theirs, near_one, near_two])
+    return call(finish_kernel, shape(bands, rows, cols), [keep, spread, known, theirs, near_one, near_two])
 
 
 def solution(mesh):

time: 19.9 us -> 17.1 us (0.86)
  local copies, waits for them, and re-layouts: 2.3 us -> 0.01 us
  starting transfers between devices: 10.3 us -> 8.29 us
  waiting for transfers between devices: 1.71 us -> 2.56 us
  Pallas kernels: 4.52 us -> 5.32 us
    unnamed x12 -> x2, local copies, waits for them, and re-layouts: 2.3 us -> 0.01 us
    ppermute x5, starting transfers between devices: 10.3 us -> 8.29 us  [swap(): return lax.ppermute(value, axes, pairs)]
    ppermute x5, waiting for transfers between devices: 1.71 us -> 2.56 us  [swap(): return lax.ppermute(value, axes, pairs)]
    pallas_call x6, Pallas kernels: 4.52 us -> 5.32 us  [call(): pl.pallas_call(kernel, out_shape=out_shape, in_specs=in_specs or [VMEM] *...]
  transfers between devices with their start and end apart: 5 -> 5, of which waited for: 3 -> 3; matrix products, arithmetic and copies ran while one was open for 0% -> 0% of each run, Pallas kernels for 18% -> 20%
where the time goes in v3:
time: 17.1 us; the launch traced here: 16.9 us
  starting transfers between devices  8.29 us (48%)
  Pallas kernels  5.32 us (31%)
  waiting for transfers between devices  2.56 us (15%)
  between operations  0.71 us (4%)
    ppermute x5, starting transfers between devices, swap(): return lax.ppermute(value, axes, pairs)  8.29 us
    pallas_call x6, Pallas kernels, call(): pl.pallas_call(kernel, out_shape=out_shape, in_specs=in_specs or [VMEM] *...  5.32 us
    ppermute x5, waiting for transfers between devices, swap(): return lax.ppermute(value, axes, pairs)  2.56 us
  transfers between devices with their start and end apart: 5, of which 3 were waited for; matrix products, arithmetic and copies ran while one was open for 0% of the time, Pallas kernels for 20%

profile of v3, /device:TPU:0, one launch (start us, length us, event | category | flops | bytes accessed | tf_op | source)
XLA Modules:
  0.0 16.9 jit_solution(13907810183245641252)
XLA Ops:
  0.0 0.0 copy-start
  0.0 1.1 %shard_map.64 = (bf16[48,128]{1,0:T(8,128)(2,1)S(1)}, bf16[8,32,128]{2,1,0:T(8,128)(2,1)S(1)}, f32[33,33]{1,0:T(8,128)S(1)}, s32[33,33]{1,0:T(8,128)S(1)}, f32[33,33]{1,0:T(8,128)S(1)}) custom-call(bf16[8,32,128]{2,1,0:T(8,128)(2,1)} %radiance.1, f32[33,33]{1,0:T(8,128)} %tap.1, s32[33,33]{1,0:T(8,128)} %sector.1, f32[33,33]{1,0:T(8,128)} %far.1), custom_call_target="tpu_custom_call" | custom-call | bytes 78604 | tf_op jit(solution)/shard_map/pallas_call | solution.py:198
  1.1 0.5 %collective-permute-start = (bf16[48,128]{1,0:T(8,128)(2,1)S(1)}, bf16[48,128]{1,0:T(8,128)(2,1)S(1)}, u32[]{:S(2)}, u32[]{:S(2)}) collective-permute-start(bf16[48,128]{1,0:T(8,128)(2,1)S(1)} %get-tuple-element.21.own_ref), channel_id=1, source_target_pairs={{0,1},{1,0},{2,3},{3,2},{4,5},{5,4},{6,7},{7,6},{8,9},{9,8},{10,11... | collective-permute-start | bytes 36872 | tf_op jit(solution)/shard_map/ppermute | solution.py:23
  2.3 0.2 %collective-permute-done.side_ref = bf16[48,128]{1,0:T(8,128)(2,1)S(1)} collective-permute-done((bf16[48,128]{1,0:T(8,128)(2,1)S(1)}, bf16[48,128]{1,0:T(8,128)(2,1)S(1)}, u32[]{:S(2)}, u32[]{:S(2)}) %collective-permute-start) | collective-permute-done | bytes 12320 | tf_op jit(solution)/shard_map/ppermute | solution.py:23
  2.5 2.9 %collective-permute-start.1 = (bf16[10,16,128]{2,1,0:T(8,128)(2,1)S(1)}, bf16[10,16,128]{2,1,0:T(8,128)(2,1)S(1)}, u32[]{:S(2)}, u32[]{:S(2)}) collective-permute-start(bf16[10,16,128]{2,1,0:T(8,128)(2,1)S(1)} %get-tuple-element.23), channel_id=1, source_target_pairs={{0,2},{2,0},{4,6},{6,4},{8,10},{10,8},{12,14},{14,12},{1,3},{3,1},... | collective-permute-start | bytes 122888 | tf_op jit(solution)/shard_map/ppermute | solution.py:23
  5.4 0.0 collective-permute-start.3
  5.4 2.0 %collective-permute-done.1.first_ref = bf16[10,16,128]{2,1,0:T(8,128)(2,1)S(1)} collective-permute-done((bf16[10,16,128]{2,1,0:T(8,128)(2,1)S(1)}, bf16[10,16,128]{2,1,0:T(8,128)(2,1)S(1)}, u32[]{:S(2)}, u32[]{:S(2)}) %collective-permute-start.1) | collective-permute-done | bytes 40992 | tf_op jit(solution)/shard_map/ppermute | solution.py:23
  7.4 2.1 %collective-permute-start.2 = (bf16[16,128]{1,0:T(8,128)(2,1)S(1)}, bf16[16,128]{1,0:T(8,128)(2,1)S(1)}, u32[]{:S(2)}, u32[]{:S(2)}) collective-permute-start(bf16[16,128]{1,0:T(8,128)(2,1)S(1)} %add_bitcast_fusion), channel_id=1, source_target_pairs={{0,4},{2,6},{4,0},{6,2},{8,12},{10,14},{12,8},{14,10},{1,5},{3,7},... | collective-permute-start | bytes 12296 | tf_op jit(solution)/shard_map/ppermute | solution.py:23
  9.5 0.0 copy-done
  9.5 0.6 %shard_map.66 = (bf16[256,1664]{1,0:T(8,128)(2,1)S(1)}, bf16[512,256]{1,0:T(8,128)(2,1)S(1)}, f32[16,32,128]{2,1,0:T(8,128)S(1)}) custom-call(f32[33,33]{1,0:T(8,128)S(1)} %get-tuple-element.25.tap_ref, s32[33,33]{1,0:T(8,128)S(1)} %get-tuple-element.26.sector_ref, f32[33,33]{1,0:T(8,128)S(1)} %get-tuple-element.27.far_ref, bf16[16,32,128]{2,1,0:T(8,128)(2,1)S(1)} %copy-done), custom_call_target="tpu_custom_call" | custom-call | flops 10000000 | bytes 144140 | tf_op jit(solution)/shard_map/pallas_call | solution.py:198
  10.1 0.0 collective-permute-done.3.second_ref
  10.1 1.4 %shard_map.67.rest_0_ = f32[4,32,128]{2,1,0:T(8,128)S(1)} custom-call(bf16[256,1664]{1,0:T(8,128)(2,1)S(1)} %get-tuple-element.30.taps_ref, bf16[8,32,128]{2,1,0:T(8,128)(2,1)S(1)} %get-tuple-element.20.radiance_ref, bf16[48,128]{1,0:T(8,128)(2,1)S(1)} %collective-permute-done.side_ref, bf16[10,16,128]{2,1,0:T(8,128)(2,1)S(1)} %collective-permute-done.1.first_ref, ...), custom_call_target="tpu_custom_call" | custom-call | flops 872415232 | bytes 1269760 | tf_op jit(solution)/shard_map/pallas_call | solution.py:198
  11.5 0.0 collective-permute-done.2
  11.5 2.8 %collective-permute-start.4 = (bf16[16,128]{1,0:T(8,128)(2,1)S(1)}, bf16[16,128]{1,0:T(8,128)(2,1)S(1)}, u32[]{:S(2)}, u32[]{:S(2)}) collective-permute-start(bf16[16,128]{1,0:T(8,128)(2,1)S(1)} %add.11.mine_ref), channel_id=1, source_target_pairs={{0,8},{2,10},{4,12},{6,14},{8,0},{10,2},{12,4},{14,6},{1,9},{3,11}... | collective-permute-start | bytes 12296 | tf_op jit(solution)/shard_map/ppermute | solution.py:23
  14.3 1.4 %shard_map.68.rest_1_ = f32[4,32,128]{2,1,0:T(8,128)S(1)} custom-call(bf16[256,1664]{1,0:T(8,128)(2,1)S(1)} %get-tuple-element.30.taps_ref, bf16[8,32,128]{2,1,0:T(8,128)(2,1)S(1)} %get-tuple-element.20.radiance_ref, bf16[48,128]{1,0:T(8,128)(2,1)S(1)} %collective-permute-done.side_ref, bf16[10,16,128]{2,1,0:T(8,128)(2,1)S(1)} %collective-permute-done.1.first_ref, ...), custom_call_target="tpu_custom_call" | custom-call | flops 872415232 | bytes 1269760 | tf_op jit(solution)/shard_map/pallas_call | solution.py:198
  15.7 0.4 %collective-permute-done.4.theirs_ref = bf16[16,128]{1,0:T(8,128)(2,1)S(1)} collective-permute-done((bf16[16,128]{1,0:T(8,128)(2,1)S(1)}, bf16[16,128]{1,0:T(8,128)(2,1)S(1)}, u32[]{:S(2)}, u32[]{:S(2)}) %collective-permute-start.4) | collective-permute-done | bytes 4128 | tf_op jit(solution)/shard_map/ppermute | solution.py:23
  16.1 0.8 %shard_map.69 = bf16[8,32,128]{2,1,0:T(8,128)(2,1)} custom-call(f32[8,128]{1,0:T(8,128)S(1)} %get-tuple-element.22.keep_ref, bf16[512,256]{1,0:T(8,128)(2,1)S(1)} %get-tuple-element.28.spread_ref, bf16[16,128]{1,0:T(8,128)(2,1)S(1)} %add.11.mine_ref, bf16[16,128]{1,0:T(8,128)(2,1)S(1)} %collective-permute-done.4.theirs_ref, ...), custom_call_target="tpu_custom_call" | custom-call | bytes 405504 | tf_op jit(solution)/shard_map/pallas_call | solution.py:198
  (3 shorter events, 0.0 us)
Async XLA Ops:
  0.0 9.5 %copy-start = (bf16[16,32,128]{2,1,0:T(8,128)(2,1)S(1)}, bf16[16,32,128]{2,1,0:T(8,128)(2,1)}, u32[]{:S(2)}) copy-start(bf16[16,32,128]{2,1,0:T(8,128)(2,1)} %sky_ref.1) | copy-start | bytes 393220
  1.1 1.3 %collective-permute-start = (bf16[48,128]{1,0:T(8,128)(2,1)S(1)}, bf16[48,128]{1,0:T(8,128)(2,1)S(1)}, u32[]{:S(2)}, u32[]{:S(2)}) collective-permute-start(bf16[48,128]{1,0:T(8,128)(2,1)S(1)} %get-tuple-element.21.own_ref), channel_id=1, source_target_pairs={{0,1},{1,0},{2,3},{3,2},{4,5},{5,4},{6,7},{7,6},{8,9},{9,8},{10,11... | collective-permute-start | bytes 36872 | tf_op jit(solution)/shard_map/ppermute | solution.py:23
  2.5 4.9 %collective-permute-start.1 = (bf16[10,16,128]{2,1,0:T(8,128)(2,1)S(1)}, bf16[10,16,128]{2,1,0:T(8,128)(2,1)S(1)}, u32[]{:S(2)}, u32[]{:S(2)}) collective-permute-start(bf16[10,16,128]{2,1,0:T(8,128)(2,1)S(1)} %get-tuple-element.23), channel_id=1, source_target_pairs={{0,2},{2,0},{4,6},{6,4},{8,10},{10,8},{12,14},{14,12},{1,3},{3,1},... | collective-permute-start | bytes 122888 | tf_op jit(solution)/shard_map/ppermute | solution.py:23
  5.4 4.7 %collective-permute-start.3 = (bf16[9,16,128]{2,1,0:T(8,128)(2,1)S(1)}, bf16[9,16,128]{2,1,0:T(8,128)(2,1)S(1)}, u32[]{:S(2)}, u32[]{:S(2)}) collective-permute-start(bf16[9,16,128]{2,1,0:T(8,128)(2,1)S(1)} %get-tuple-element.31), channel_id=1, source_target_pairs={{0,1},{1,0},{2,4},{3,5},{4,2},{5,3},{6,8},{7,9},{8,6},{9,7},{10,12... | collective-permute-start | bytes 110600 | tf_op jit(solution)/shard_map/ppermute | solution.py:23
  7.4 4.1 %collective-permute-start.2 = (bf16[16,128]{1,0:T(8,128)(2,1)S(1)}, bf16[16,128]{1,0:T(8,128)(2,1)S(1)}, u32[]{:S(2)}, u32[]{:S(2)}) collective-permute-start(bf16[16,128]{1,0:T(8,128)(2,1)S(1)} %add_bitcast_fusion), channel_id=1, source_target_pairs={{0,4},{2,6},{4,0},{6,2},{8,12},{10,14},{12,8},{14,10},{1,5},{3,7},... | collective-permute-start | bytes 12296 | tf_op jit(solution)/shard_map/ppermute | solution.py:23
  11.5 4.6 %collective-permute-start.4 = (bf16[16,128]{1,0:T(8,128)(2,1)S(1)}, bf16[16,128]{1,0:T(8,128)(2,1)S(1)}, u32[]{:S(2)}, u32[]{:S(2)}) collective-permute-start(bf16[16,128]{1,0:T(8,128)(2,1)S(1)} %add.11.mine_ref), channel_id=1, source_target_pairs={{0,8},{2,10},{4,12},{6,14},{8,0},{10,2},{12,4},{14,6},{1,9},{3,11}... | collective-permute-start | bytes 12296 | tf_op jit(solution)/shard_map/ppermute | solution.py:23

commit v4 on v3

--- a/solution.py
+++ b/solution.py
@@ -29,47 +29,43 @@
     return lax.ppermute(value, axis, [(source, source + steps) for source in range(leading, last)])
 
 
-def prepare_kernel(radiance, tap, sector, far, message_ref, radiance_ref, tap_ref, sector_ref, far_ref, sems):
-    pairs = [(radiance, radiance_ref), (tap, tap_ref), (sector, sector_ref), (far, far_ref)]
-    fetches = [pltpu.make_async_copy(*pair, sems.at[k]) for k, pair in enumerate(pairs)]
+def fetch_kernel(*refs):
+    half = len(refs) // 2
+    sems = refs[-1]
+    fetches = [pltpu.make_async_copy(refs[k], refs[half + k], sems.at[k]) for k in range(half)]
     for fetch in fetches:
         fetch.start()
+    for fetch in fetches:
+        fetch.wait()
+
+
+def pack_kernel(radiance_ref, other_ref, first_ref, second_ref, side_ref):
     row, col = lax.axis_index("row"), lax.axis_index("col")
     bands, rows, cols = radiance_ref.shape
-    fetches[0].wait()
     height = rows // DEC
-    cells = radiance_ref[...].reshape(bands * rows, cols)
-    place = (iota((cols, 256), 0) >> 4) + col * (cols // DEC)
-    chooser = ((iota((cols, 256), 1) >> 4) == place).astype(BF16)
-    sums = jnp.dot(cells, chooser, preferred_element_type=F32)
-    sums = jnp.sum(sums.reshape(bands, height, DEC, 256), axis=2)
+    known = jnp.zeros((bands, 256), F32)
     own_row = (iota((bands, height, 256), 2) & 15) - iota((bands, height, 256), 1)
-    coarse = jnp.sum(jnp.where(own_row == row * height, sums, 0.0), axis=1) * (1.0 / (DEC * DEC))
-    coarse = jnp.concatenate([coarse[:, :LANES], coarse[:, LANES:]], axis=0)
-    message_ref[rows : rows + 2 * bands, :] = coarse.astype(BF16)
+    offset = (iota((cols, 256), 1) >> 4) - (iota((cols, 256), 0) >> 4)
+    for ref, which in ((radiance_ref, col), (other_ref, 1 - col)):
+        chooser = (offset == which * (cols // DEC)).astype(BF16)
+        sums = jnp.dot(ref[...].reshape(bands * rows, cols), chooser, preferred_element_type=F32)
+        sums = jnp.sum(sums.reshape(bands, height, DEC, 256), axis=2)
+        known = known + jnp.sum(jnp.where(own_row == row * height, sums, 0.0), axis=1)
+    known = known * (1.0 / (DEC * DEC))
+    first_ref[bands + 1] = jnp.concatenate([known[:, :LANES], known[:, LANES:]], axis=0).astype(BF16)
     lane = iota((rows, cols), 1)
     packed = jnp.zeros((rows, cols), F32)
     for b in range(bands):
-        moved = pltpu.roll(radiance_ref[b].astype(F32), 16 * b, 1)
-        first = 16 * b - 16 * (1 - col)
-        packed = jnp.where(((lane - first) & (cols - 1)) < 16, moved, packed)
-    message_ref[0:rows, :] = packed.astype(BF16)
-    for fetch in fetches[1:]:
-        fetch.wait()
-
-
-def pack_kernel(land_ref, radiance_ref, own_ref, side_ref, first_ref, second_ref, keep_ref):
-    bands, rows, cols = radiance_ref.shape
-    odd = lax.axis_index("row") & 1
+        moved = pltpu.roll(other_ref[b].astype(F32), 16 * b, 1)
+        packed = jnp.where(((lane - (16 * b - 16 * col)) & (cols - 1)) < 16, moved, packed)
+    side_ref[...] = packed.astype(BF16)
+    odd = row & 1
     near = pl.multiple_of(STEP * (1 - odd), STEP)
     away = pl.multiple_of(STEP * odd, STEP)
     first_ref[0:bands] = radiance_ref[:, pl.ds(near, STEP), :]
     first_ref[bands] = side_ref[pl.ds(near, STEP), :]
-    first_ref[bands + 1] = own_ref[rows : rows + 16, :] + side_ref[rows : rows + 16, :]
     second_ref[0:bands] = radiance_ref[:, pl.ds(away, STEP), :]
     second_ref[bands] = side_ref[pl.ds(away, STEP), :]
-    ones = jnp.ones(keep_ref.shape, F32)
-    keep_ref[...] = jnp.where(land_ref[0, 0] > 0, ones, jnp.zeros_like(ones))
 
 
 def weights_kernel(
@@ -119,58 +115,58 @@
     view_ref[...] = sky_ref[...].astype(F32)
 
 
-def near_kernel(offset, taps_ref, radiance_ref, side_ref, first_ref, second_ref, sky_ref, near_ref, tiles):
+def near_kernel(second, taps_ref, radiance_ref, side_ref, strip_ref, sky_ref, near_ref, tiles):
     row, col, last = lax.axis_index("row"), lax.axis_index("col"), lax.axis_size("row") - 1
     bands, rows, cols = radiance_ref.shape
     sectors = sky_ref.shape[0]
     span = 33
     reach = 16
     tall = STEP + span - 1
-    odd = (row & 1) == 1
-    keep_up = row > 0
-    keep_low = row < last
+    odd = row & 1
+    above = (odd == 0) if second else (odd == 1)
     tiles[:, span * tall :, :] = jnp.zeros((2, tiles.shape[1] - span * tall, tiles.shape[2]), BF16)
-    zero = jnp.zeros((STEP, cols), F32)
 
     def around(b, middle):
-        one = first_ref[b].astype(F32)
-        two = second_ref[b].astype(F32)
-        up = jnp.where(keep_up, jnp.where(odd, one, two), zero)
-        low = jnp.where(keep_low, jnp.where(odd, two, one), zero)
-        return jnp.concatenate([up, middle.astype(F32), low], axis=0)
-
-    packed = around(bands, side_ref[0:rows, :])
+        strip = strip_ref[b].astype(F32)
+        if second:
+            strip = jnp.where(inside, strip, jnp.zeros_like(strip))
+        middle = middle.astype(F32)
+        upper = jnp.concatenate([strip, middle], axis=0)
+        return jnp.where(above, upper, jnp.concatenate([middle, strip], axis=0))
+
+    inside = jnp.where(above, row, last - row) > 0
+    packed = around(bands, side_ref[...])
     lane = iota(packed.shape, 1)
     edge = jnp.where(col == 0, (lane < reach).astype(F32), (lane >= cols - reach).astype(F32))
-    for n in range(near_ref.shape[0]):
-        b = offset + n
-        own = around(b, radiance_ref[b])
-        aux = pltpu.roll(packed, (cols - 16 * b) % cols, 1) * edge
-        slot = n % 2
-        for d in range(span):
-            shift = d - reach
-            if shift > 0:
-                value = jnp.where(lane < shift, aux, own)
-            elif shift < 0:
-                value = jnp.where(lane >= cols + shift, aux, own)
-            else:
-                value = own
-            if shift:
-                value = pltpu.roll(value, (cols - shift) % cols, 1)
-            value = value.astype(BF16)
-            for i in range(2):
-                tiles[slot, d * tall : (d + 1) * tall, i * cols : (i + 1) * cols] = value[i * STEP : i * STEP + tall]
+    start = pl.multiple_of(jnp.where(above, 0, STEP), STEP)
+    for pair in range(bands // 2):
+        slot = pair % 2
+        for k in range(2):
+            b = 2 * pair + k
+            own = around(b, radiance_ref[b])
+            aux = pltpu.roll(packed, (cols - 16 * b) % cols, 1) * edge
+            for d in range(span):
+                shift = d - reach
+                if shift > 0:
+                    value = jnp.where(lane < shift, aux, own)
+                elif shift < 0:
+                    value = jnp.where(lane >= cols + shift, aux, own)
+                else:
+                    value = own
+                if shift:
+                    value = pltpu.roll(value, (cols - shift) % cols, 1)
+                tiles[slot, d * tall : (d + 1) * tall, k * cols : (k + 1) * cols] = value.astype(BF16)
         sums = jnp.dot(taps_ref[...], tiles[slot], preferred_element_type=F32)
-        for i in range(2):
-            part = sums[:, i * cols : (i + 1) * cols].reshape(sectors, STEP, cols)
-            sky = sky_ref[:, i * STEP : (i + 1) * STEP, :]
-            near_ref[n, i * STEP : (i + 1) * STEP, :] = jnp.sum(part * sky, axis=0)
-
-
-def finish_kernel(keep_ref, spread_ref, mine_ref, theirs_ref, *rest):
-    near_refs, out_ref = rest[:-1], rest[-1]
+        sky = sky_ref[:, pl.ds(start, STEP), :]
+        for k in range(2):
+            part = sums[:, k * cols : (k + 1) * cols].reshape(sectors, STEP, cols)
+            near_ref[2 * pair + k] = jnp.sum(part * sky, axis=0)
+
+
+def finish_kernel(keep_ref, spread_ref, mine_ref, theirs_ref, one_ref, two_ref, out_ref):
+    odd = (lax.axis_index("row") & 1) == 1
+    land = keep_ref[0:1, :] > 0
     bands = out_ref.shape[0]
-    land = keep_ref[0:1, :] > 0
     if mine_ref.shape[0] == 2 * bands:
         known = mine_ref[...].astype(F32) + theirs_ref[...].astype(F32)
         known = jnp.concatenate([known[:bands], known[bands:]], axis=1)
@@ -178,14 +174,10 @@
         known = mine_ref[...].astype(F32)
     known = jnp.concatenate([known, known], axis=1).astype(BF16)
     far = jnp.dot(known, spread_ref[...], preferred_element_type=F32)
-    at = 0
-    for near_ref in near_refs:
-        count = near_ref.shape[0]
-        for i in range(2):
-            block = far[at : at + count, i * LANES : (i + 1) * LANES][:, None, :]
-            total = near_ref[:, i * DEC : (i + 1) * DEC, :] + block
-            out_ref[at : at + count, i * DEC : (i + 1) * DEC, :] = jnp.where(land, total, 0.0).astype(BF16)
-        at += count
+    one, two = one_ref[...], two_ref[...]
+    for i, near in enumerate((jnp.where(odd, one, two), jnp.where(odd, two, one))):
+        total = near + far[:, i * LANES : (i + 1) * LANES][:, None, :]
+        out_ref[:, i * DEC : (i + 1) * DEC, :] = jnp.where(land, total, 0.0).astype(BF16)
 
 
 VMEM = pl.BlockSpec(memory_space=pltpu.VMEM)
@@ -240,33 +232,35 @@
         return jax.ShapeDtypeStruct(dims, kind)
 
     inputs = [radiance, tap_weight, tap_sector, far_weight]
-    message, radiance, tap_weight, tap_sector, far_weight = call(
-        prepare_kernel,
-        [shape(rows + 16, LANES)] + [jax.ShapeDtypeStruct(a.shape, a.dtype) for a in inputs],
+    other = swap(radiance, "col", [(0, 1), (1, 0)])
+    own, tap_weight, tap_sector, far_weight = call(
+        fetch_kernel,
+        [jax.ShapeDtypeStruct(a.shape, a.dtype) for a in inputs],
         [pltpu.with_memory_space_constraint(a, pltpu.HBM) for a in inputs],
         [pltpu.SemaphoreType.DMA((len(inputs),))],
         in_specs=[HBM] * len(inputs),
     )
-    side = swap(message, "col", [(0, 1), (1, 0)])
-    first, second, keep = call(
+    first, second, side = call(
         pack_kernel,
-        (shape(bands + 2, STEP, LANES), shape(bands + 1, STEP, LANES), shape(8, LANES, kind=F32)),
-        [land_mask, radiance, message, side],
-        in_specs=[SMEM] + [VMEM] * 3,
+        (
+            shape(bands + 2, STEP, LANES),
+            shape(bands + 1, STEP, LANES),
+            shape(rows, LANES),
+        ),
+        [own, other],
     )
 
     def flat(r, c):
         return r * n_col + c
 
-    def other(r, c):
+    def beyond(r, c):
         q = r + 1 if r % 2 else r - 1
         return flat(q, c) if 0 <= q < n_row else flat(r, 1 - c)
 
     everyone = [(r, c) for r in range(n_row) for c in range(n_col)]
     from_first = swap(first, "row", [(r, r ^ 1) for r in range(n_row)])
-    from_second = swap(second, ("row", "col"), [(flat(r, c), other(r, c)) for r, c in everyone])
-
-    from_first, tap_weight = lax.optimization_barrier((from_first, tap_weight))
+    from_second = swap(second, ("row", "col"), [(flat(r, c), beyond(r, c)) for r, c in everyone])
+
     height = 16 if compact else 48
     tall = span + STEP - 1
     wide = -(-span * tall // LANES) * LANES
@@ -277,20 +271,20 @@
         [pltpu.VMEM((2 * tall, LANES), F32), pltpu.VMEM((64, LANES), F32)],
         flops=10_000_000,
     )
-    def near(at, count):
+    def near(second, strips):
         return call(
-            functools.partial(near_kernel, at),
-            shape(count, rows, cols, kind=F32),
-            [taps, radiance, side, from_first, from_second, sky],
+            functools.partial(near_kernel, second),
+            shape(bands, STEP, cols, kind=F32),
+            [taps, own, side, strips, sky],
             [pltpu.VMEM((2, wide, 2 * cols), BF16)],
-            flops=2 * sectors * STEP * wide * 2 * cols * count,
+            flops=sectors * STEP * wide * 2 * cols * bands,
         )
 
-    half = bands // 2
+    keep = jnp.broadcast_to((land_mask[0, 0] > 0).astype(F32), (8, LANES))
     if compact:
         known = first[bands + 1] + from_first[bands + 1]
         theirs = swap(known, "row", [(r, r ^ 2) for r in range(n_row)])
-        near_one = near(0, half)
+        near_one = near(False, from_first)
         theirs, near_one = lax.optimization_barrier((theirs, near_one))
         step = 4
         while step < n_row:
@@ -298,11 +292,11 @@
             theirs = swap(known, "row", [(r, r ^ step) for r in range(n_row)])
             step *= 2
     else:
-        near_one = near(0, half)
+        near_one = near(False, from_first)
         window = coarse_window(radiance, far_reach)
         window = jnp.pad(window, ((0, 0), (0, 0), (0, height - window.shape[2])))
         known = theirs = window.reshape(bands, all_cols * height)
-    near_two = near(half, bands - half)
+    near_two = near(True, from_second)
     return call(finish_kernel, shape(bands, rows, cols), [keep, spread, known, theirs, near_one, near_two])
 
 

time: 17.1 us -> 16.2 us (0.947)
  waiting for transfers between devices: 2.56 us -> 0.84 us
  Pallas kernels: 5.32 us -> 6.15 us
    ppermute x5, waiting for transfers between devices: 2.56 us -> 0.84 us  [swap(): return lax.ppermute(value, axes, pairs)]
    pallas_call x6, Pallas kernels: 5.32 us -> 6.15 us  [call(): pl.pallas_call(kernel, out_shape=out_shape, in_specs=in_specs or [VMEM] *...]
  transfers between devices with their start and end apart: 5 -> 5, of which waited for: 3 -> 2; matrix products, arithmetic and copies ran while one was open for 0% -> 0% of each run, Pallas kernels for 20% -> 31%
where the time goes in v4:
time: 16.2 us; the launch traced here: 16.1 us
  starting transfers between devices  8.35 us (52%)
  Pallas kernels  6.15 us (38%)
  waiting for transfers between devices  0.84 us (5%)
  between operations  0.74 us (5%)
    ppermute x5, starting transfers between devices, swap(): return lax.ppermute(value, axes, pairs)  8.35 us
    pallas_call x6, Pallas kernels, call(): pl.pallas_call(kernel, out_shape=out_shape, in_specs=in_specs or [VMEM] *...  6.15 us
    ppermute x5, waiting for transfers between devices, swap(): return lax.ppermute(value, axes, pairs)  0.84 us
  transfers between devices with their start and end apart: 5, of which 2 were waited for; matrix products, arithmetic and copies ran while one was open for 0% of the time, Pallas kernels for 31%

profile of v4, /device:TPU:0, one launch (start us, length us, event | category | flops | bytes accessed | tf_op | source)
XLA Modules:
  0.0 16.1 jit_solution(2672969799615052352)
XLA Ops:
  0.0 0.0 copy-start
  0.0 0.5 %collective-permute-start = (bf16[8,32,128]{2,1,0:T(8,128)(2,1)}, bf16[8,32,128]{2,1,0:T(8,128)(2,1)S(1)}, u32[]{:S(2)}, u32[]{:S(2)}) collective-permute-start(bf16[8,32,128]{2,1,0:T(8,128)(2,1)} %refs_0_.1), channel_id=1, source_target_pairs={{0,1},{1,0},{2,3},{3,2},{4,5},{5,4},{6,7},{7,6},{8,9},{9,8},{10,11... | collective-permute-start | bytes 196616 | tf_op jit(solution)/shard_map/ppermute | solution.py:23
  0.5 0.9 %shard_map.64 = (bf16[8,32,128]{2,1,0:T(8,128)(2,1)S(1)}, f32[33,33]{1,0:T(8,128)S(1)}, s32[33,33]{1,0:T(8,128)S(1)}, f32[33,33]{1,0:T(8,128)S(1)}) custom-call(bf16[8,32,128]{2,1,0:T(8,128)(2,1)} %refs_0_.1, f32[33,33]{1,0:T(8,128)} %refs_1_.1, s32[33,33]{1,0:T(8,128)} %refs_2_.1, f32[33,33]{1,0:T(8,128)} %refs_3_.1), custom_call_target="tpu_custom_call" | custom-call | bytes 78604 | tf_op jit(solution)/shard_map/pallas_call | solution.py:190
  1.3 0.2 %collective-permute-done.other_ref = bf16[8,32,128]{2,1,0:T(8,128)(2,1)S(1)} collective-permute-done((bf16[8,32,128]{2,1,0:T(8,128)(2,1)}, bf16[8,32,128]{2,1,0:T(8,128)(2,1)S(1)}, u32[]{:S(2)}, u32[]{:S(2)}) %collective-permute-start) | collective-permute-done | bytes 65568 | tf_op jit(solution)/shard_map/ppermute | solution.py:23
  1.6 0.3 %shard_map.66 = (bf16[10,16,128]{2,1,0:T(8,128)(2,1)S(1)}, bf16[9,16,128]{2,1,0:T(8,128)(2,1)S(1)}, bf16[32,128]{1,0:T(8,128)(2,1)S(1)}) custom-call(bf16[8,32,128]{2,1,0:T(8,128)(2,1)S(1)} %get-tuple-element.21.radiance_ref, bf16[8,32,128]{2,1,0:T(8,128)(2,1)S(1)} %collective-permute-done.other_ref), custom_call_target="tpu_custom_call" | custom-call | bytes 131072 | tf_op jit(solution)/shard_map/pallas_call | solution.py:190
  1.9 2.9 %collective-permute-start.1 = (bf16[10,16,128]{2,1,0:T(8,128)(2,1)S(1)}, bf16[10,16,128]{2,1,0:T(8,128)(2,1)S(1)}, u32[]{:S(2)}, u32[]{:S(2)}) collective-permute-start(bf16[10,16,128]{2,1,0:T(8,128)(2,1)S(1)} %get-tuple-element.22), channel_id=1, source_target_pairs={{0,2},{2,0},{4,6},{6,4},{8,10},{10,8},{12,14},{14,12},{1,3},{3,1},... | collective-permute-start | bytes 122888 | tf_op jit(solution)/shard_map/ppermute | solution.py:23
  5.4 0.0 copy-done
  5.4 0.6 %shard_map.65 = (bf16[256,1664]{1,0:T(8,128)(2,1)S(1)}, bf16[512,256]{1,0:T(8,128)(2,1)S(1)}, f32[16,32,128]{2,1,0:T(8,128)S(1)}) custom-call(f32[33,33]{1,0:T(8,128)S(1)} %get-tuple-element.17.tap_ref, s32[33,33]{1,0:T(8,128)S(1)} %get-tuple-element.18.sector_ref, f32[33,33]{1,0:T(8,128)S(1)} %get-tuple-element.19.far_ref, bf16[16,32,128]{2,1,0:T(8,128)(2,1)S(1)} %copy-done), custom_call_target="tpu_custom_call" | custom-call | flops 10000000 | bytes 144140 | tf_op jit(solution)/shard_map/pallas_call | solution.py:190
  6.1 0.1 collective-permute-start.4
  6.1 0.6 %collective-permute-done.1.strip_ref = bf16[10,16,128]{2,1,0:T(8,128)(2,1)S(1)} collective-permute-done((bf16[10,16,128]{2,1,0:T(8,128)(2,1)S(1)}, bf16[10,16,128]{2,1,0:T(8,128)(2,1)S(1)}, u32[]{:S(2)}, u32[]{:S(2)}) %collective-permute-start.1) | collective-permute-done | bytes 40992 | tf_op jit(solution)/shard_map/ppermute | solution.py:23
  6.7 2.1 %collective-permute-start.2 = (bf16[16,128]{1,0:T(8,128)(2,1)S(1)}, bf16[16,128]{1,0:T(8,128)(2,1)S(1)}, u32[]{:S(2)}, u32[]{:S(2)}) collective-permute-start(bf16[16,128]{1,0:T(8,128)(2,1)S(1)} %fusion), channel_id=1, source_target_pairs={{0,4},{2,6},{4,0},{6,2},{8,12},{10,14},{12,8},{14,10},{1,5},{3,7},... | collective-permute-start | bytes 12296 | tf_op jit(solution)/shard_map/ppermute | solution.py:23
  8.9 1.8 %shard_map.67.one_ref = f32[8,16,128]{2,1,0:T(8,128)S(1)} custom-call(bf16[256,1664]{1,0:T(8,128)(2,1)S(1)} %get-tuple-element.23.taps_ref, bf16[8,32,128]{2,1,0:T(8,128)(2,1)S(1)} %get-tuple-element.21.radiance_ref, bf16[32,128]{1,0:T(8,128)(2,1)S(1)} %get-tuple-element.24.side_ref, bf16[10,16,128]{2,1,0:T(8,128)(2,1)S(1)} %collective-permute-done.1.strip_ref, ...), custom_call_target="tpu_custom_call" | custom-call | flops 872415232 | bytes 1228800 | tf_op jit(solution)/shard_map/pallas_call | solution.py:190
  10.6 0.0 collective-permute-done.2
  10.7 2.8 %collective-permute-start.3 = (bf16[16,128]{1,0:T(8,128)(2,1)S(1)}, bf16[16,128]{1,0:T(8,128)(2,1)S(1)}, u32[]{:S(2)}, u32[]{:S(2)}) collective-permute-start(bf16[16,128]{1,0:T(8,128)(2,1)S(1)} %add.11.mine_ref), channel_id=1, source_target_pairs={{0,8},{2,10},{4,12},{6,14},{8,0},{10,2},{12,4},{14,6},{1,9},{3,11}... | collective-permute-start | bytes 12296 | tf_op jit(solution)/shard_map/ppermute | solution.py:23
  13.5 0.0 collective-permute-done.4.strip_ref
  13.5 1.8 %shard_map.68.two_ref = f32[8,16,128]{2,1,0:T(8,128)S(1)} custom-call(bf16[256,1664]{1,0:T(8,128)(2,1)S(1)} %get-tuple-element.23.taps_ref, bf16[8,32,128]{2,1,0:T(8,128)(2,1)S(1)} %get-tuple-element.21.radiance_ref, bf16[32,128]{1,0:T(8,128)(2,1)S(1)} %get-tuple-element.24.side_ref, bf16[9,16,128]{2,1,0:T(8,128)(2,1)S(1)} %collective-permute-done.4.strip_ref, ...), custom_call_target="tpu_custom_call" | custom-call | flops 872415232 | bytes 1224704 | tf_op jit(solution)/shard_map/pallas_call | solution.py:190
  15.3 0.0 collective-permute-done.3.theirs_ref
  15.3 0.8 %shard_map.69 = bf16[8,32,128]{2,1,0:T(8,128)(2,1)} custom-call(f32[8,128]{1,0:T(8,128)S(1)} %broadcast_in_dim.3.keep_ref, bf16[512,256]{1,0:T(8,128)(2,1)S(1)} %get-tuple-element.20.spread_ref, bf16[16,128]{1,0:T(8,128)(2,1)S(1)} %add.11.mine_ref, bf16[16,128]{1,0:T(8,128)(2,1)S(1)} %collective-permute-done.3.theirs_ref, ...), custom_call_target="tpu_custom_call" | custom-call | bytes 405504 | tf_op jit(solution)/shard_map/pallas_call | solution.py:190
  (3 shorter events, 0.0 us)
Async XLA Ops:
  0.0 5.4 %copy-start = (bf16[16,32,128]{2,1,0:T(8,128)(2,1)S(1)}, bf16[16,32,128]{2,1,0:T(8,128)(2,1)}, u32[]{:S(2)}) copy-start(bf16[16,32,128]{2,1,0:T(8,128)(2,1)} %sky_ref.1) | copy-start | bytes 393220
  0.0 1.6 %collective-permute-start = (bf16[8,32,128]{2,1,0:T(8,128)(2,1)}, bf16[8,32,128]{2,1,0:T(8,128)(2,1)S(1)}, u32[]{:S(2)}, u32[]{:S(2)}) collective-permute-start(bf16[8,32,128]{2,1,0:T(8,128)(2,1)} %refs_0_.1), channel_id=1, source_target_pairs={{0,1},{1,0},{2,3},{3,2},{4,5},{5,4},{6,7},{7,6},{8,9},{9,8},{10,11... | collective-permute-start | bytes 196616 | tf_op jit(solution)/shard_map/ppermute | solution.py:23
  1.9 4.9 %collective-permute-start.1 = (bf16[10,16,128]{2,1,0:T(8,128)(2,1)S(1)}, bf16[10,16,128]{2,1,0:T(8,128)(2,1)S(1)}, u32[]{:S(2)}, u32[]{:S(2)}) collective-permute-start(bf16[10,16,128]{2,1,0:T(8,128)(2,1)S(1)} %get-tuple-element.22), channel_id=1, source_target_pairs={{0,2},{2,0},{4,6},{6,4},{8,10},{10,8},{12,14},{14,12},{1,3},{3,1},... | collective-permute-start | bytes 122888 | tf_op jit(solution)/shard_map/ppermute | solution.py:23
  6.1 7.4 %collective-permute-start.4 = (bf16[9,16,128]{2,1,0:T(8,128)(2,1)S(1)}, bf16[9,16,128]{2,1,0:T(8,128)(2,1)S(1)}, u32[]{:S(2)}, u32[]{:S(2)}) collective-permute-start(bf16[9,16,128]{2,1,0:T(8,128)(2,1)S(1)} %get-tuple-element.28), channel_id=1, source_target_pairs={{0,1},{1,0},{2,4},{3,5},{4,2},{5,3},{6,8},{7,9},{8,6},{9,7},{10,12... | collective-permute-start | bytes 110600 | tf_op jit(solution)/shard_map/ppermute | solution.py:23
  6.7 3.9 %collective-permute-start.2 = (bf16[16,128]{1,0:T(8,128)(2,1)S(1)}, bf16[16,128]{1,0:T(8,128)(2,1)S(1)}, u32[]{:S(2)}, u32[]{:S(2)}) collective-permute-start(bf16[16,128]{1,0:T(8,128)(2,1)S(1)} %fusion), channel_id=1, source_target_pairs={{0,4},{2,6},{4,0},{6,2},{8,12},{10,14},{12,8},{14,10},{1,5},{3,7},... | collective-permute-start | bytes 12296 | tf_op jit(solution)/shard_map/ppermute | solution.py:23
  10.7 4.6 %collective-permute-start.3 = (bf16[16,128]{1,0:T(8,128)(2,1)S(1)}, bf16[16,128]{1,0:T(8,128)(2,1)S(1)}, u32[]{:S(2)}, u32[]{:S(2)}) collective-permute-start(bf16[16,128]{1,0:T(8,128)(2,1)S(1)} %add.11.mine_ref), channel_id=1, source_target_pairs={{0,8},{2,10},{4,12},{6,14},{8,0},{10,2},{12,4},{14,6},{1,9},{3,11}... | collective-permute-start | bytes 12296 | tf_op jit(solution)/shard_map/ppermute | solution.py:23

commit v5 on v4

--- a/solution.py
+++ b/solution.py
@@ -17,10 +17,6 @@
 
 def iota(shape, axis):
     return lax.broadcasted_iota(I32, shape, axis)
-
-
-def swap(value, axes, pairs):
-    return lax.ppermute(value, axes, pairs)
 
 
 def shifted(value, axis, steps):
@@ -39,7 +35,7 @@
         fetch.wait()
 
 
-def pack_kernel(radiance_ref, other_ref, first_ref, second_ref, side_ref):
+def pack_kernel(radiance_ref, other_ref, first_ref, second_ref, side_ref, corner_s):
     row, col = lax.axis_index("row"), lax.axis_index("col")
     bands, rows, cols = radiance_ref.shape
     height = rows // DEC
@@ -54,18 +50,23 @@
     known = known * (1.0 / (DEC * DEC))
     first_ref[bands + 1] = jnp.concatenate([known[:, :LANES], known[:, LANES:]], axis=0).astype(BF16)
     lane = iota((rows, cols), 1)
-    packed = jnp.zeros((rows, cols), F32)
-    for b in range(bands):
-        moved = pltpu.roll(other_ref[b].astype(F32), 16 * b, 1)
-        packed = jnp.where(((lane - (16 * b - 16 * col)) & (cols - 1)) < 16, moved, packed)
-    side_ref[...] = packed.astype(BF16)
+
+    def edges(ref, side_col):
+        packed = jnp.zeros((rows, cols), F32)
+        for b in range(bands):
+            moved = pltpu.roll(ref[b].astype(F32), 16 * b, 1)
+            packed = jnp.where(((lane - (16 * b - 16 * side_col)) & (cols - 1)) < 16, moved, packed)
+        return packed.astype(BF16)
+
+    side_ref[...] = edges(other_ref, col)
+    corner_s[...] = edges(radiance_ref, 1 - col)
     odd = row & 1
     near = pl.multiple_of(STEP * (1 - odd), STEP)
     away = pl.multiple_of(STEP * odd, STEP)
-    first_ref[0:bands] = radiance_ref[:, pl.ds(near, STEP), :]
-    first_ref[bands] = side_ref[pl.ds(near, STEP), :]
-    second_ref[0:bands] = radiance_ref[:, pl.ds(away, STEP), :]
-    second_ref[bands] = side_ref[pl.ds(away, STEP), :]
+    first_ref[0:bands] = other_ref[:, pl.ds(near, STEP), :]
+    first_ref[bands] = corner_s[pl.ds(near, STEP), :]
+    second_ref[0:bands] = other_ref[:, pl.ds(away, STEP), :]
+    second_ref[bands] = corner_s[pl.ds(away, STEP), :]
 
 
 def weights_kernel(
@@ -232,7 +233,7 @@
         return jax.ShapeDtypeStruct(dims, kind)
 
     inputs = [radiance, tap_weight, tap_sector, far_weight]
-    other = swap(radiance, "col", [(0, 1), (1, 0)])
+    other = lax.ppermute(radiance, "col", [(0, 1), (1, 0)])
     own, tap_weight, tap_sector, far_weight = call(
         fetch_kernel,
         [jax.ShapeDtypeStruct(a.shape, a.dtype) for a in inputs],
@@ -248,18 +249,21 @@
             shape(rows, LANES),
         ),
         [own, other],
+        [pltpu.VMEM((rows, cols), BF16)],
     )
 
-    def flat(r, c):
-        return r * n_col + c
-
-    def beyond(r, c):
+    everyone = [(r, c) for r in range(n_row) for c in range(n_col)]
+
+    def crossing(value, partner):
+        pairs = [(r * n_col + c, partner(r) * n_col + 1 - c) for r, c in everyone]
+        return lax.ppermute(value, ("row", "col"), pairs)
+
+    def beyond(r):
         q = r + 1 if r % 2 else r - 1
-        return flat(q, c) if 0 <= q < n_row else flat(r, 1 - c)
-
-    everyone = [(r, c) for r in range(n_row) for c in range(n_col)]
-    from_first = swap(first, "row", [(r, r ^ 1) for r in range(n_row)])
-    from_second = swap(second, ("row", "col"), [(flat(r, c), beyond(r, c)) for r, c in everyone])
+        return q if 0 <= q < n_row else r
+
+    from_first = crossing(first, lambda r: r ^ 1)
+    from_second = crossing(second, beyond)
 
     height = 16 if compact else 48
     tall = span + STEP - 1
@@ -283,13 +287,13 @@
     keep = jnp.broadcast_to((land_mask[0, 0] > 0).astype(F32), (8, LANES))
     if compact:
         known = first[bands + 1] + from_first[bands + 1]
-        theirs = swap(known, "row", [(r, r ^ 2) for r in range(n_row)])
+        theirs = crossing(known, lambda r: r ^ 2)
         near_one = near(False, from_first)
         theirs, near_one = lax.optimization_barrier((theirs, near_one))
         step = 4
         while step < n_row:
             known = known + theirs
-            theirs = swap(known, "row", [(r, r ^ step) for r in range(n_row)])
+            theirs = crossing(known, lambda r, k=step: r ^ k)
             step *= 2
     else:
         near_one = near(False, from_first)

time: 16.2 us -> 15.3 us (0.944)
  waiting for transfers between devices: 0.84 us -> 0.24 us
  starting transfers between devices: 8.35 us -> 8.04 us
    ppermute x5, waiting for transfers between devices: 0.84 us -> 0.24 us  [the longest x1 0.23 us: body(): other = lax.ppermute(radiance, 'col', [(0, 1), (1, 0)])]
    ppermute x5, starting transfers between devices: 8.35 us -> 8.04 us  [the longest x4 7.59 us: crossing(): return lax.ppermute(value, ('row', 'col'), pairs)]
  transfers between devices with their start and end apart: 5 -> 5, of which waited for: 2 -> 1; matrix products, arithmetic and copies ran while one was open for 0% -> 0% of each run, Pallas kernels for 31% -> 33%
where the time goes in v5:
time: 15.3 us; the launch traced here: 15.2 us
  starting transfers between devices  8.04 us (53%)
  Pallas kernels  6.15 us (40%)
  between operations  0.74 us (5%)
  waiting for transfers between devices  0.24 us (2%)
    ppermute x4, starting transfers between devices, crossing(): return lax.ppermute(value, ('row', 'col'), pairs)  7.59 us
    pallas_call x6, Pallas kernels, call(): pl.pallas_call(kernel, out_shape=out_shape, in_specs=in_specs or [VMEM] *...  6.15 us
    ppermute x1, starting transfers between devices, body(): other = lax.ppermute(radiance, 'col', [(0, 1), (1, 0)])  0.45 us
  transfers between devices with their start and end apart: 5, of which 1 were waited for; matrix products, arithmetic and copies ran while one was open for 0% of the time, Pallas kernels for 33%

profile of v5, /device:TPU:0, one launch (start us, length us, event | category | flops | bytes accessed | tf_op | source)
XLA Modules:
  0.0 15.2 jit_solution(12412604603498894769)
XLA Ops:
  0.0 0.0 copy-start
  0.0 0.5 %collective-permute-start = (bf16[8,32,128]{2,1,0:T(8,128)(2,1)}, bf16[8,32,128]{2,1,0:T(8,128)(2,1)S(1)}, u32[]{:S(2)}, u32[]{:S(2)}) collective-permute-start(bf16[8,32,128]{2,1,0:T(8,128)(2,1)} %refs_0_.1), channel_id=1, source_target_pairs={{0,1},{1,0},{2,3},{3,2},{4,5},{5,4},{6,7},{7,6},{8,9},{9,8},{10,11... | collective-permute-start | bytes 196616 | tf_op jit(solution)/shard_map/ppermute | solution.py:236
  0.5 0.9 %shard_map.64 = (bf16[8,32,128]{2,1,0:T(8,128)(2,1)S(1)}, f32[33,33]{1,0:T(8,128)S(1)}, s32[33,33]{1,0:T(8,128)S(1)}, f32[33,33]{1,0:T(8,128)S(1)}) custom-call(bf16[8,32,128]{2,1,0:T(8,128)(2,1)} %refs_0_.1, f32[33,33]{1,0:T(8,128)} %refs_1_.1, s32[33,33]{1,0:T(8,128)} %refs_2_.1, f32[33,33]{1,0:T(8,128)} %refs_3_.1), custom_call_target="tpu_custom_call" | custom-call | bytes 78604 | tf_op jit(solution)/shard_map/pallas_call | solution.py:191
  1.3 0.2 %collective-permute-done.other_ref = bf16[8,32,128]{2,1,0:T(8,128)(2,1)S(1)} collective-permute-done((bf16[8,32,128]{2,1,0:T(8,128)(2,1)}, bf16[8,32,128]{2,1,0:T(8,128)(2,1)S(1)}, u32[]{:S(2)}, u32[]{:S(2)}) %collective-permute-start) | collective-permute-done | bytes 65568 | tf_op jit(solution)/shard_map/ppermute | solution.py:236
  1.6 0.3 %shard_map.66 = (bf16[10,16,128]{2,1,0:T(8,128)(2,1)S(1)}, bf16[9,16,128]{2,1,0:T(8,128)(2,1)S(1)}, bf16[32,128]{1,0:T(8,128)(2,1)S(1)}) custom-call(bf16[8,32,128]{2,1,0:T(8,128)(2,1)S(1)} %get-tuple-element.21.radiance_ref, bf16[8,32,128]{2,1,0:T(8,128)(2,1)S(1)} %collective-permute-done.other_ref), custom_call_target="tpu_custom_call" | custom-call | bytes 131072 | tf_op jit(solution)/shard_map/pallas_call | solution.py:191
  1.9 2.7 %collective-permute-start.1 = (bf16[10,16,128]{2,1,0:T(8,128)(2,1)S(1)}, bf16[10,16,128]{2,1,0:T(8,128)(2,1)S(1)}, u32[]{:S(2)}, u32[]{:S(2)}) collective-permute-start(bf16[10,16,128]{2,1,0:T(8,128)(2,1)S(1)} %get-tuple-element.22), channel_id=1, source_target_pairs={{0,3},{1,2},{2,1},{3,0},{4,7},{5,6},{6,5},{7,4},{8,11},{9,10},{10,... | collective-permute-start | bytes 122888 | tf_op jit(solution)/shard_map/ppermute | solution.py:259
  5.2 0.0 copy-done
  5.2 0.6 %shard_map.65 = (bf16[256,1664]{1,0:T(8,128)(2,1)S(1)}, bf16[512,256]{1,0:T(8,128)(2,1)S(1)}, f32[16,32,128]{2,1,0:T(8,128)S(1)}) custom-call(f32[33,33]{1,0:T(8,128)S(1)} %get-tuple-element.17.tap_ref, s32[33,33]{1,0:T(8,128)S(1)} %get-tuple-element.18.sector_ref, f32[33,33]{1,0:T(8,128)S(1)} %get-tuple-element.19.far_ref, bf16[16,32,128]{2,1,0:T(8,128)(2,1)S(1)} %copy-done), custom_call_target="tpu_custom_call" | custom-call | flops 10000000 | bytes 144140 | tf_op jit(solution)/shard_map/pallas_call | solution.py:191
  5.8 0.4 %collective-permute-start.4 = (bf16[9,16,128]{2,1,0:T(8,128)(2,1)S(1)}, bf16[9,16,128]{2,1,0:T(8,128)(2,1)S(1)}, u32[]{:S(2)}, u32[]{:S(2)}) collective-permute-start(bf16[9,16,128]{2,1,0:T(8,128)(2,1)S(1)} %get-tuple-element.28), channel_id=1, source_target_pairs={{0,1},{1,0},{2,5},{3,4},{4,3},{5,2},{6,9},{7,8},{8,7},{9,6},{10,13... | collective-permute-start | bytes 110600 | tf_op jit(solution)/shard_map/ppermute | solution.py:259
  6.2 0.0 collective-permute-done.1.strip_ref
  6.3 1.9 %collective-permute-start.2 = (bf16[16,128]{1,0:T(8,128)(2,1)S(1)}, bf16[16,128]{1,0:T(8,128)(2,1)S(1)}, u32[]{:S(2)}, u32[]{:S(2)}) collective-permute-start(bf16[16,128]{1,0:T(8,128)(2,1)S(1)} %fusion), channel_id=1, source_target_pairs={{0,5},{1,4},{2,7},{3,6},{4,1},{5,0},{6,3},{7,2},{8,13},{9,12},{10,... | collective-permute-start | bytes 12296 | tf_op jit(solution)/shard_map/ppermute | solution.py:259
  8.2 1.8 %shard_map.67.one_ref = f32[8,16,128]{2,1,0:T(8,128)S(1)} custom-call(bf16[256,1664]{1,0:T(8,128)(2,1)S(1)} %get-tuple-element.23.taps_ref, bf16[8,32,128]{2,1,0:T(8,128)(2,1)S(1)} %get-tuple-element.21.radiance_ref, bf16[32,128]{1,0:T(8,128)(2,1)S(1)} %get-tuple-element.24.side_ref, bf16[10,16,128]{2,1,0:T(8,128)(2,1)S(1)} %collective-permute-done.1.strip_ref, ...), custom_call_target="tpu_custom_call" | custom-call | flops 872415232 | bytes 1228800 | tf_op jit(solution)/shard_map/pallas_call | solution.py:191
  9.9 0.0 collective-permute-done.2
  10.0 2.6 %collective-permute-start.3 = (bf16[16,128]{1,0:T(8,128)(2,1)S(1)}, bf16[16,128]{1,0:T(8,128)(2,1)S(1)}, u32[]{:S(2)}, u32[]{:S(2)}) collective-permute-start(bf16[16,128]{1,0:T(8,128)(2,1)S(1)} %add.11.mine_ref), channel_id=1, source_target_pairs={{0,9},{1,8},{2,11},{3,10},{4,13},{5,12},{6,15},{7,14},{8,1},{9,0},... | collective-permute-start | bytes 12296 | tf_op jit(solution)/shard_map/ppermute | solution.py:259
  12.6 0.0 collective-permute-done.4.strip_ref
  12.6 1.8 %shard_map.68.two_ref = f32[8,16,128]{2,1,0:T(8,128)S(1)} custom-call(bf16[256,1664]{1,0:T(8,128)(2,1)S(1)} %get-tuple-element.23.taps_ref, bf16[8,32,128]{2,1,0:T(8,128)(2,1)S(1)} %get-tuple-element.21.radiance_ref, bf16[32,128]{1,0:T(8,128)(2,1)S(1)} %get-tuple-element.24.side_ref, bf16[9,16,128]{2,1,0:T(8,128)(2,1)S(1)} %collective-permute-done.4.strip_ref, ...), custom_call_target="tpu_custom_call" | custom-call | flops 872415232 | bytes 1224704 | tf_op jit(solution)/shard_map/pallas_call | solution.py:191
  14.4 0.0 collective-permute-done.3.theirs_ref
  14.4 0.8 %shard_map.69 = bf16[8,32,128]{2,1,0:T(8,128)(2,1)} custom-call(f32[8,128]{1,0:T(8,128)S(1)} %broadcast_in_dim.3.keep_ref, bf16[512,256]{1,0:T(8,128)(2,1)S(1)} %get-tuple-element.20.spread_ref, bf16[16,128]{1,0:T(8,128)(2,1)S(1)} %add.11.mine_ref, bf16[16,128]{1,0:T(8,128)(2,1)S(1)} %collective-permute-done.3.theirs_ref, ...), custom_call_target="tpu_custom_call" | custom-call | bytes 405504 | tf_op jit(solution)/shard_map/pallas_call | solution.py:191
  (3 shorter events, 0.0 us)
Async XLA Ops:
  0.0 5.2 %copy-start = (bf16[16,32,128]{2,1,0:T(8,128)(2,1)S(1)}, bf16[16,32,128]{2,1,0:T(8,128)(2,1)}, u32[]{:S(2)}) copy-start(bf16[16,32,128]{2,1,0:T(8,128)(2,1)} %sky_ref.1) | copy-start | bytes 393220
  0.0 1.6 %collective-permute-start = (bf16[8,32,128]{2,1,0:T(8,128)(2,1)}, bf16[8,32,128]{2,1,0:T(8,128)(2,1)S(1)}, u32[]{:S(2)}, u32[]{:S(2)}) collective-permute-start(bf16[8,32,128]{2,1,0:T(8,128)(2,1)} %refs_0_.1), channel_id=1, source_target_pairs={{0,1},{1,0},{2,3},{3,2},{4,5},{5,4},{6,7},{7,6},{8,9},{9,8},{10,11... | collective-permute-start | bytes 196616 | tf_op jit(solution)/shard_map/ppermute | solution.py:236
  1.9 4.4 %collective-permute-start.1 = (bf16[10,16,128]{2,1,0:T(8,128)(2,1)S(1)}, bf16[10,16,128]{2,1,0:T(8,128)(2,1)S(1)}, u32[]{:S(2)}, u32[]{:S(2)}) collective-permute-start(bf16[10,16,128]{2,1,0:T(8,128)(2,1)S(1)} %get-tuple-element.22), channel_id=1, source_target_pairs={{0,3},{1,2},{2,1},{3,0},{4,7},{5,6},{6,5},{7,4},{8,11},{9,10},{10,... | collective-permute-start | bytes 122888 | tf_op jit(solution)/shard_map/ppermute | solution.py:259
  5.8 6.7 %collective-permute-start.4 = (bf16[9,16,128]{2,1,0:T(8,128)(2,1)S(1)}, bf16[9,16,128]{2,1,0:T(8,128)(2,1)S(1)}, u32[]{:S(2)}, u32[]{:S(2)}) collective-permute-start(bf16[9,16,128]{2,1,0:T(8,128)(2,1)S(1)} %get-tuple-element.28), channel_id=1, source_target_pairs={{0,1},{1,0},{2,5},{3,4},{4,3},{5,2},{6,9},{7,8},{8,7},{9,6},{10,13... | collective-permute-start | bytes 110600 | tf_op jit(solution)/shard_map/ppermute | solution.py:259
  6.3 3.7 %collective-permute-start.2 = (bf16[16,128]{1,0:T(8,128)(2,1)S(1)}, bf16[16,128]{1,0:T(8,128)(2,1)S(1)}, u32[]{:S(2)}, u32[]{:S(2)}) collective-permute-start(bf16[16,128]{1,0:T(8,128)(2,1)S(1)} %fusion), channel_id=1, source_target_pairs={{0,5},{1,4},{2,7},{3,6},{4,1},{5,0},{6,3},{7,2},{8,13},{9,12},{10,... | collective-permute-start | bytes 12296 | tf_op jit(solution)/shard_map/ppermute | solution.py:259
  10.0 4.4 %collective-permute-start.3 = (bf16[16,128]{1,0:T(8,128)(2,1)S(1)}, bf16[16,128]{1,0:T(8,128)(2,1)S(1)}, u32[]{:S(2)}, u32[]{:S(2)}) collective-permute-start(bf16[16,128]{1,0:T(8,128)(2,1)S(1)} %add.11.mine_ref), channel_id=1, source_target_pairs={{0,9},{1,8},{2,11},{3,10},{4,13},{5,12},{6,15},{7,14},{8,1},{9,0},... | collective-permute-start | bytes 12296 | tf_op jit(solution)/shard_map/ppermute | solution.py:259

commit v6 on v5

--- a/solution.py
+++ b/solution.py
@@ -70,7 +70,7 @@
 
 
 def weights_kernel(
-    height, whole_grid, tap_ref, sector_ref, far_ref, sky_ref, taps_ref, spread_ref, view_ref, tap_s, far_s
+    height, whole_grid, tap_ref, sector_ref, far_ref, sky_ref, taps_ref, spread_ref, view_ref, tap_s, turned_s, far_s
 ):
     row, col = lax.axis_index("row"), lax.axis_index("col")
     span = tap_ref.shape[0]
@@ -78,24 +78,36 @@
     wide = taps_ref.shape[1]
     sectors = taps_ref.shape[0] // STEP
     tap_s[...] = jnp.zeros(tap_s.shape, F32)
-    tap_s[0:span, 0:span] = tap_ref[...]
-    tap_s[tall : tall + span, 0:span] = sector_ref[...].astype(F32)
-    lane = iota((LANES, wide), 1) - tall * iota((LANES, wide), 0)
-    pick = ((lane >= 0) & (lane < tall)).astype(BF16)
-    both = jnp.dot(tap_s[...].astype(BF16), pick, preferred_element_type=F32)
-    which = iota((tall, wide), 1) % tall == iota((tall, wide), 0)
-    weight = jnp.sum(jnp.where(which, both[0:tall], 0.0), axis=0, keepdims=True)
-    sector = jnp.sum(jnp.where(which, both[tall:], 0.0), axis=0, keepdims=True)
-    weight = pltpu.roll(jnp.broadcast_to(weight, (STEP, wide)), 0, 1, stride=1, stride_axis=0)
-    sector = pltpu.roll(jnp.broadcast_to(sector, (STEP, wide)), 0, 1, stride=1, stride_axis=0)
+    tap_s[0, 0:span, 0:span] = tap_ref[...]
+    tap_s[1, 0:span, 0:span] = sector_ref[...].astype(F32)
+    lane = iota((STEP, LANES), 1)
+    chunks = [[jnp.zeros((STEP, LANES), F32)] * (wide // LANES) for _ in range(2)]
+    for which in range(2):
+        turned_s[which] = tap_s[which].T
+        for d in range(span):
+            at = d * tall
+            row_d = jnp.broadcast_to(turned_s[which, d : d + 1, :], (STEP, LANES))
+            moved = pltpu.roll(row_d, at % LANES, 1, stride=1, stride_axis=0)
+            first, last = at // LANES, (at + tall - 1) // LANES
+            if first == last:
+                inside = (lane >= at % LANES) & (lane < at % LANES + tall)
+                chunks[which][first] = jnp.where(inside, moved, chunks[which][first])
+            else:
+                chunks[which][first] = jnp.where(lane >= at % LANES, moved, chunks[which][first])
+                chunks[which][last] = jnp.where(lane < (at + tall) % LANES, moved, chunks[which][last])
+    weight = [chunk.astype(BF16) for chunk in chunks[0]]
+    sector = [chunk.astype(BF16) for chunk in chunks[1]]
+    none = jnp.zeros((STEP, LANES), BF16)
     for s in range(sectors):
-        taps_ref[s * STEP : (s + 1) * STEP, :] = jnp.where(sector == s, weight, 0.0).astype(BF16)
+        for k in range(wide // LANES):
+            tile = jnp.where(sector[k] == jnp.array(s, BF16), weight[k], none)
+            taps_ref[s * STEP : (s + 1) * STEP, k * LANES : (k + 1) * LANES] = tile
     far_s[...] = jnp.zeros(far_s.shape, F32)
     far_s[8 : 8 + span, 0:span] = far_ref[...]
     reach = (span - 1) // 2
     coarse_cols = LANES // DEC
     all_cols = spread_ref.shape[0] // (2 * height)
-    lane = iota((LANES, all_cols * LANES), 1)
+    lane = iota((1, all_cols * LANES), 1)
     want = (lane >> 7) - coarse_cols * col - ((lane & (LANES - 1)) >> 4) + reach
     pick = (iota((LANES, all_cols * LANES), 0) == want).astype(BF16)
     parts = []
@@ -128,17 +140,16 @@
     tiles[:, span * tall :, :] = jnp.zeros((2, tiles.shape[1] - span * tall, tiles.shape[2]), BF16)
 
     def around(b, middle):
-        strip = strip_ref[b].astype(F32)
+        strip = strip_ref[b]
         if second:
             strip = jnp.where(inside, strip, jnp.zeros_like(strip))
-        middle = middle.astype(F32)
         upper = jnp.concatenate([strip, middle], axis=0)
         return jnp.where(above, upper, jnp.concatenate([middle, strip], axis=0))
 
     inside = jnp.where(above, row, last - row) > 0
     packed = around(bands, side_ref[...])
     lane = iota(packed.shape, 1)
-    edge = jnp.where(col == 0, (lane < reach).astype(F32), (lane >= cols - reach).astype(F32))
+    edge = jnp.where(col == 0, (lane < reach).astype(F32), (lane >= cols - reach).astype(F32)).astype(BF16)
     start = pl.multiple_of(jnp.where(above, 0, STEP), STEP)
     for pair in range(bands // 2):
         slot = pair % 2
@@ -156,7 +167,7 @@
                     value = own
                 if shift:
                     value = pltpu.roll(value, (cols - shift) % cols, 1)
-                tiles[slot, d * tall : (d + 1) * tall, k * cols : (k + 1) * cols] = value.astype(BF16)
+                tiles[slot, d * tall : (d + 1) * tall, k * cols : (k + 1) * cols] = value
         sums = jnp.dot(taps_ref[...], tiles[slot], preferred_element_type=F32)
         sky = sky_ref[:, pl.ds(start, STEP), :]
         for k in range(2):
@@ -241,6 +252,17 @@
         [pltpu.SemaphoreType.DMA((len(inputs),))],
         in_specs=[HBM] * len(inputs),
     )
+    height = 16 if compact else 48
+    tall = span + STEP - 1
+    wide = -(-span * tall // LANES) * LANES
+    taps, spread, sky = call(
+        functools.partial(weights_kernel, height, compact),
+        (shape(sectors * STEP, wide), shape(2 * all_cols * height, 2 * LANES), shape(sectors, rows, cols, kind=F32)),
+        [tap_weight, tap_sector, far_weight, sky_view],
+        [pltpu.VMEM((2, LANES, LANES), F32), pltpu.VMEM((2, LANES, LANES), F32), pltpu.VMEM((64, LANES), F32)],
+        flops=10_000_000,
+    )
+    other, taps, spread, sky = lax.optimization_barrier((other, taps, spread, sky))
     first, second, side = call(
         pack_kernel,
         (
@@ -265,16 +287,6 @@
     from_first = crossing(first, lambda r: r ^ 1)
     from_second = crossing(second, beyond)
 
-    height = 16 if compact else 48
-    tall = span + STEP - 1
-    wide = -(-span * tall // LANES) * LANES
-    taps, spread, sky = call(
-        functools.partial(weights_kernel, height, compact),
-        (shape(sectors * STEP, wide), shape(2 * all_cols * height, 2 * LANES), shape(sectors, rows, cols, kind=F32)),
-        [tap_weight, tap_sector, far_weight, sky_view],
-        [pltpu.VMEM((2 * tall, LANES), F32), pltpu.VMEM((64, LANES), F32)],
-        flops=10_000_000,
-    )
     def near(second, strips):
         return call(
             functools.partial(near_kernel, second),

time: 15.3 us -> 15 us (0.980)
  waiting for transfers between devices: 0.24 us -> 1.04 us
  starting transfers between devices: 8.04 us -> 7.39 us
  Pallas kernels: 6.15 us -> 5.64 us
    ppermute x4, waiting for transfers between devices: 0.01 us -> 1.04 us  [crossing(): return lax.ppermute(value, ('row', 'col'), pairs)]
    ppermute x4, starting transfers between devices: 7.59 us -> 6.94 us  [crossing(): return lax.ppermute(value, ('row', 'col'), pairs)]
    pallas_call x6, Pallas kernels: 6.15 us -> 5.64 us  [call(): pl.pallas_call(kernel, out_shape=out_shape, in_specs=in_specs or [VMEM] *...]
    ppermute x1, waiting for transfers between devices: 0.23 us -> 0.01 us  [body(): other = lax.ppermute(radiance, 'col', [(0, 1), (1, 0)])]
  transfers between devices with their start and end apart: 5 -> 5, of which waited for: 1 -> 1; matrix products, arithmetic and copies ran while one was open for 0% -> 0% of each run, Pallas kernels for 33% -> 31%
where the time goes in v6:
time: 15 us; the launch traced here: 14.8 us
  starting transfers between devices  7.39 us (49%)
  Pallas kernels  5.64 us (38%)
  waiting for transfers between devices  1.04 us (7%)
  between operations  0.75 us (5%)
    ppermute x4, starting transfers between devices, crossing(): return lax.ppermute(value, ('row', 'col'), pairs)  6.94 us
    pallas_call x6, Pallas kernels, call(): pl.pallas_call(kernel, out_shape=out_shape, in_specs=in_specs or [VMEM] *...  5.64 us
    ppermute x4, waiting for transfers between devices, crossing(): return lax.ppermute(value, ('row', 'col'), pairs)  1.04 us
    ppermute x1, starting transfers between devices, body(): other = lax.ppermute(radiance, 'col', [(0, 1), (1, 0)])  0.45 us
  transfers between devices with their start and end apart: 5, of which 1 were waited for; matrix products, arithmetic and copies ran while one was open for 0% of the time, Pallas kernels for 31%

profile of v6, /device:TPU:0, one launch (start us, length us, event | category | flops | bytes accessed | tf_op | source)
XLA Modules:
  0.0 14.8 jit_solution(251236297311331177)
XLA Ops:
  0.0 0.0 copy-start
  0.0 0.5 %collective-permute-start = (bf16[8,32,128]{2,1,0:T(8,128)(2,1)}, bf16[8,32,128]{2,1,0:T(8,128)(2,1)S(1)}, u32[]{:S(2)}, u32[]{:S(2)}) collective-permute-start(bf16[8,32,128]{2,1,0:T(8,128)(2,1)} %refs_0_.1), channel_id=1, source_target_pairs={{0,1},{1,0},{2,3},{3,2},{4,5},{5,4},{6,7},{7,6},{8,9},{9,8},{10,11... | collective-permute-start | bytes 196616 | tf_op jit(solution)/shard_map/ppermute | solution.py:247
  0.5 0.9 %shard_map.64 = (bf16[8,32,128]{2,1,0:T(8,128)(2,1)S(1)}, f32[33,33]{1,0:T(8,128)S(1)}, s32[33,33]{1,0:T(8,128)S(1)}, f32[33,33]{1,0:T(8,128)S(1)}) custom-call(bf16[8,32,128]{2,1,0:T(8,128)(2,1)} %refs_0_.1, f32[33,33]{1,0:T(8,128)} %refs_1_.1, s32[33,33]{1,0:T(8,128)} %refs_2_.1, f32[33,33]{1,0:T(8,128)} %refs_3_.1), custom_call_target="tpu_custom_call" | custom-call | bytes 78604 | tf_op jit(solution)/shard_map/pallas_call | solution.py:202
  1.3 0.0 copy-done
  1.4 0.5 %shard_map.65 = (bf16[256,1664]{1,0:T(8,128)(2,1)S(1)}, bf16[512,256]{1,0:T(8,128)(2,1)S(1)}, f32[16,32,128]{2,1,0:T(8,128)S(1)}) custom-call(f32[33,33]{1,0:T(8,128)S(1)} %get-tuple-element.21.tap_ref, s32[33,33]{1,0:T(8,128)S(1)} %get-tuple-element.22.sector_ref, f32[33,33]{1,0:T(8,128)S(1)} %get-tuple-element.23.far_ref, bf16[16,32,128]{2,1,0:T(8,128)(2,1)S(1)} %copy-done), custom_call_target="tpu_custom_call" | custom-call | flops 10000000 | bytes 144140 | tf_op jit(solution)/shard_map/pallas_call | solution.py:202
  1.8 0.0 collective-permute-done.other_ref
  1.8 0.3 %shard_map.66 = (bf16[10,16,128]{2,1,0:T(8,128)(2,1)S(1)}, bf16[9,16,128]{2,1,0:T(8,128)(2,1)S(1)}, bf16[32,128]{1,0:T(8,128)(2,1)S(1)}) custom-call(bf16[8,32,128]{2,1,0:T(8,128)(2,1)S(1)} %get-tuple-element.28.radiance_ref, bf16[8,32,128]{2,1,0:T(8,128)(2,1)S(1)} %collective-permute-done.other_ref), custom_call_target="tpu_custom_call" | custom-call | bytes 131072 | tf_op jit(solution)/shard_map/pallas_call | solution.py:202
  2.1 2.7 %collective-permute-start.1 = (bf16[10,16,128]{2,1,0:T(8,128)(2,1)S(1)}, bf16[10,16,128]{2,1,0:T(8,128)(2,1)S(1)}, u32[]{:S(2)}, u32[]{:S(2)}) collective-permute-start(bf16[10,16,128]{2,1,0:T(8,128)(2,1)S(1)} %get-tuple-element.30), channel_id=1, source_target_pairs={{0,3},{1,2},{2,1},{3,0},{4,7},{5,6},{6,5},{7,4},{8,11},{9,10},{10,... | collective-permute-start | bytes 122888 | tf_op jit(solution)/shard_map/ppermute | solution.py:281
  5.5 0.1 collective-permute-start.4
  5.6 1.0 %collective-permute-done.1.strip_ref = bf16[10,16,128]{2,1,0:T(8,128)(2,1)S(1)} collective-permute-done((bf16[10,16,128]{2,1,0:T(8,128)(2,1)S(1)}, bf16[10,16,128]{2,1,0:T(8,128)(2,1)S(1)}, u32[]{:S(2)}, u32[]{:S(2)}) %collective-permute-start.1) | collective-permute-done | bytes 40992 | tf_op jit(solution)/shard_map/ppermute | solution.py:281
  6.6 1.7 %collective-permute-start.2 = (bf16[16,128]{1,0:T(8,128)(2,1)S(1)}, bf16[16,128]{1,0:T(8,128)(2,1)S(1)}, u32[]{:S(2)}, u32[]{:S(2)}) collective-permute-start(bf16[16,128]{1,0:T(8,128)(2,1)S(1)} %fusion), channel_id=1, source_target_pairs={{0,5},{1,4},{2,7},{3,6},{4,1},{5,0},{6,3},{7,2},{8,13},{9,12},{10,... | collective-permute-start | bytes 12296 | tf_op jit(solution)/shard_map/ppermute | solution.py:281
  8.3 1.6 %shard_map.67.one_ref = f32[8,16,128]{2,1,0:T(8,128)S(1)} custom-call(bf16[256,1664]{1,0:T(8,128)(2,1)S(1)} %get-tuple-element.31.taps_ref, bf16[8,32,128]{2,1,0:T(8,128)(2,1)S(1)} %get-tuple-element.28.radiance_ref, bf16[32,128]{1,0:T(8,128)(2,1)S(1)} %get-tuple-element.32.side_ref, bf16[10,16,128]{2,1,0:T(8,128)(2,1)S(1)} %collective-permute-done.1.strip_ref, ...), custom_call_target="tpu_custom_call" | custom-call | flops 872415232 | bytes 1228800 | tf_op jit(solution)/shard_map/pallas_call | solution.py:202
  9.9 0.0 collective-permute-done.2
  10.0 2.4 %collective-permute-start.3 = (bf16[16,128]{1,0:T(8,128)(2,1)S(1)}, bf16[16,128]{1,0:T(8,128)(2,1)S(1)}, u32[]{:S(2)}, u32[]{:S(2)}) collective-permute-start(bf16[16,128]{1,0:T(8,128)(2,1)S(1)} %add.11.mine_ref), channel_id=1, source_target_pairs={{0,9},{1,8},{2,11},{3,10},{4,13},{5,12},{6,15},{7,14},{8,1},{9,0},... | collective-permute-start | bytes 12296 | tf_op jit(solution)/shard_map/ppermute | solution.py:281
  12.4 0.0 collective-permute-done.4.strip_ref
  12.4 1.6 %shard_map.68.two_ref = f32[8,16,128]{2,1,0:T(8,128)S(1)} custom-call(bf16[256,1664]{1,0:T(8,128)(2,1)S(1)} %get-tuple-element.31.taps_ref, bf16[8,32,128]{2,1,0:T(8,128)(2,1)S(1)} %get-tuple-element.28.radiance_ref, bf16[32,128]{1,0:T(8,128)(2,1)S(1)} %get-tuple-element.32.side_ref, bf16[9,16,128]{2,1,0:T(8,128)(2,1)S(1)} %collective-permute-done.4.strip_ref, ...), custom_call_target="tpu_custom_call" | custom-call | flops 872415232 | bytes 1224704 | tf_op jit(solution)/shard_map/pallas_call | solution.py:202
  14.0 0.0 collective-permute-done.3.theirs_ref
  14.0 0.8 %shard_map.69 = bf16[8,32,128]{2,1,0:T(8,128)(2,1)} custom-call(f32[8,128]{1,0:T(8,128)S(1)} %broadcast_in_dim.3.keep_ref, bf16[512,256]{1,0:T(8,128)(2,1)S(1)} %get-tuple-element.27.spread_ref, bf16[16,128]{1,0:T(8,128)(2,1)S(1)} %add.11.mine_ref, bf16[16,128]{1,0:T(8,128)(2,1)S(1)} %collective-permute-done.3.theirs_ref, ...), custom_call_target="tpu_custom_call" | custom-call | bytes 405504 | tf_op jit(solution)/shard_map/pallas_call | solution.py:202
  (3 shorter events, 0.0 us)
Async XLA Ops:
  0.0 1.3 %copy-start = (bf16[16,32,128]{2,1,0:T(8,128)(2,1)S(1)}, bf16[16,32,128]{2,1,0:T(8,128)(2,1)}, u32[]{:S(2)}) copy-start(bf16[16,32,128]{2,1,0:T(8,128)(2,1)} %sky_ref.1) | copy-start | bytes 393220
  0.0 1.8 %collective-permute-start = (bf16[8,32,128]{2,1,0:T(8,128)(2,1)}, bf16[8,32,128]{2,1,0:T(8,128)(2,1)S(1)}, u32[]{:S(2)}, u32[]{:S(2)}) collective-permute-start(bf16[8,32,128]{2,1,0:T(8,128)(2,1)} %refs_0_.1), channel_id=1, source_target_pairs={{0,1},{1,0},{2,3},{3,2},{4,5},{5,4},{6,7},{7,6},{8,9},{9,8},{10,11... | collective-permute-start | bytes 196616 | tf_op jit(solution)/shard_map/ppermute | solution.py:247
  2.1 4.5 %collective-permute-start.1 = (bf16[10,16,128]{2,1,0:T(8,128)(2,1)S(1)}, bf16[10,16,128]{2,1,0:T(8,128)(2,1)S(1)}, u32[]{:S(2)}, u32[]{:S(2)}) collective-permute-start(bf16[10,16,128]{2,1,0:T(8,128)(2,1)S(1)} %get-tuple-element.30), channel_id=1, source_target_pairs={{0,3},{1,2},{2,1},{3,0},{4,7},{5,6},{6,5},{7,4},{8,11},{9,10},{10,... | collective-permute-start | bytes 122888 | tf_op jit(solution)/shard_map/ppermute | solution.py:281
  5.5 6.9 %collective-permute-start.4 = (bf16[9,16,128]{2,1,0:T(8,128)(2,1)S(1)}, bf16[9,16,128]{2,1,0:T(8,128)(2,1)S(1)}, u32[]{:S(2)}, u32[]{:S(2)}) collective-permute-start(bf16[9,16,128]{2,1,0:T(8,128)(2,1)S(1)} %get-tuple-element.36), channel_id=1, source_target_pairs={{0,1},{1,0},{2,5},{3,4},{4,3},{5,2},{6,9},{7,8},{8,7},{9,6},{10,13... | collective-permute-start | bytes 110600 | tf_op jit(solution)/shard_map/ppermute | solution.py:281
  6.6 3.3 %collective-permute-start.2 = (bf16[16,128]{1,0:T(8,128)(2,1)S(1)}, bf16[16,128]{1,0:T(8,128)(2,1)S(1)}, u32[]{:S(2)}, u32[]{:S(2)}) collective-permute-start(bf16[16,128]{1,0:T(8,128)(2,1)S(1)} %fusion), channel_id=1, source_target_pairs={{0,5},{1,4},{2,7},{3,6},{4,1},{5,0},{6,3},{7,2},{8,13},{9,12},{10,... | collective-permute-start | bytes 12296 | tf_op jit(solution)/shard_map/ppermute | solution.py:281
  10.0 4.0 %collective-permute-start.3 = (bf16[16,128]{1,0:T(8,128)(2,1)S(1)}, bf16[16,128]{1,0:T(8,128)(2,1)S(1)}, u32[]{:S(2)}, u32[]{:S(2)}) collective-permute-start(bf16[16,128]{1,0:T(8,128)(2,1)S(1)} %add.11.mine_ref), channel_id=1, source_target_pairs={{0,9},{1,8},{2,11},{3,10},{4,13},{5,12},{6,15},{7,14},{8,1},{9,0},... | collective-permute-start | bytes 12296 | tf_op jit(solution)/shard_map/ppermute | solution.py:281
